TPU v7x, 32 devices: a whole 2x2x4 slice. The times are simulated.
32 devices in a mesh: gx: 8 (over y, x, core), gy: 4 (over z).
Axes of the slice: x: 2, y: 2, z: 4, core: 2. Of those that a mesh axis runs over, the one named last changes fastest.
Arguments:
- control: float32 [3, 64, 256, 1024], P(None, None, 'gy', 'gx')
- spread: float32 [3, 256, 1024], P(None, 'gy', 'gx'), may hold values from 0.5 to 2
- kernel_east: float32 [3, 9], replicated, may hold values from -1.5 to 1.5
- kernel_north: float32 [3, 9], replicated, may hold values from -1.5 to 1.5
- vertical: float32 [3, 64, 64], replicated, may hold values from -0.75 to 0.75
- tile_owner: int32 [16384], P(('gx', 'gy')), may hold values from 0 to 31, as said below
- gate_level: int32 [16384], P(('gx', 'gy')), may hold values from 0 to 63
- tile_row: int32 [16384], P(('gx', 'gy')), may hold values from 0 to 63
- beam_azimuth: int32 [16384], P(('gx', 'gy')), may hold values from 80 to 280, as said below
- innovation: float32 [16384, 2, 128], P(('gx', 'gy')), may hold values from -6 to 6
- obs_weight: float32 [16384, 2, 128], P(('gx', 'gy')), may hold values from 0.25 to 4
Outputs:
- gradient: float32 [3, 64, 256, 1024], P(None, None, 'gy', 'gx')
- cost: float32 [2], replicated
Inputs may be any that keep to these rules, and one draw needn't show every extreme that they name: `tile_owner`: among the gate rows of one device no tile is named more than 32 times; one tile is named exactly 32 times by the rows of every device. `beam_azimuth`: every azimuth lies within 10 degrees of due east (90) or due west (270).
All inputs are finite; a program needn't handle non-finite values.
Results may differ from a plain program's by a relative error of at most 0.00009.
Values sent between devices are 32-bit elements; how exact they have to be, the bound alone decides.
A program may use at most 192 MiB of HBM per device.

v0:
```python
import math

import jax
import jax.numpy as jnp
from jax import lax
from jax.sharding import PartitionSpec as P

HIGHEST = lax.Precision.HIGHEST


def padded(block, sides, width):
    for axis, dim in sides:
        count = lax.axis_size(axis)
        forward = [(i, i + 1) for i in range(count - 1)]
        backward = [(target, source) for source, target in forward]
        low = lax.ppermute(
            lax.slice_in_dim(block, block.shape[dim] - width, None, axis=dim), axis, forward
        )
        high = lax.ppermute(lax.slice_in_dim(block, 0, width, axis=dim), axis, backward)
        block = jnp.concatenate([low, block, high], axis=dim)
    return block


def band_matrix(kernel, length):
    reach = kernel.shape[1] - 1
    weights = jnp.concatenate([kernel[:, ::-1], kernel[:, 1:]], axis=1)
    offset = lax.broadcasted_iota(
        jnp.int32, (length + 2 * reach, length), 0
    ) - lax.broadcasted_iota(jnp.int32, (length + 2 * reach, length), 1)
    picks = (
        offset[None, :, :] == lax.broadcasted_iota(jnp.int32, (2 * reach + 1, 1, 1), 0)
    ).astype(jnp.float32)
    return jnp.einsum("fk,kjl->fjl", weights, picks, precision=HIGHEST)


def smooth(field, east_band, north_band, reach):
    widened = padded(field, (("gx", 3),), reach)
    flatter = jnp.einsum("fzyj,fji->fzyi", widened, east_band, precision=HIGHEST)
    across = padded(flatter, (("gy", 2),), reach)
    return jnp.einsum("fzjx,fji->fzix", across, north_band, precision=HIGHEST)


def route_rows(payload, labels):
    return (
        lax.all_to_all(payload, ("gx", "gy"), split_axis=0, concat_axis=0, tiled=True),
        lax.all_to_all(labels, ("gx", "gy"), split_axis=0, concat_axis=0, tiled=True),
    )


def body(
    control,
    spread,
    kernel_east,
    kernel_north,
    vertical,
    tile_owner,
    gate_level,
    tile_row,
    beam_azimuth,
    innovation,
    obs_weight,
):
    fields, levels, rows_tile, cols_tile = control.shape
    reach = kernel_east.shape[1] - 1
    tiles = lax.axis_size("gx") * lax.axis_size("gy")
    rows_dev = tile_owner.shape[0]
    most = 2 * rows_dev // tiles
    hits = (tile_owner[:, None] == jnp.arange(tiles, dtype=jnp.int32)[None, :]).astype(jnp.int32)
    rank = jnp.sum((jnp.cumsum(hits, axis=0) - 1) * hits, axis=1)
    slot = tile_owner * most + rank
    payload = (
        jnp.zeros((tiles * most, 4, cols_tile), jnp.float32)
        .at[slot]
        .set(jnp.concatenate([innovation, obs_weight], axis=1))
    )
    labels = (
        jnp.zeros((tiles * most, 3), jnp.int32)
        .at[slot]
        .set(jnp.stack([gate_level, tile_row, beam_azimuth], axis=1))
    )
    arrived, arrived_labels = route_rows(payload, labels)
    east_band = band_matrix(kernel_east, cols_tile)
    north_band = band_matrix(kernel_north, rows_tile)
    smoothed = smooth(control, east_band, north_band, reach)
    state_field = spread[:, None] * jnp.einsum(
        "fkz,fzyx->fkyx", vertical, smoothed, precision=HIGHEST
    )
    row_index = arrived_labels[:, 0] * rows_tile + arrived_labels[:, 1]
    flat_state = state_field.reshape(fields, levels * rows_tile, cols_tile)
    picked = flat_state[:, row_index, :]
    angle = arrived_labels[:, 2].astype(jnp.float32) * (2.0 * math.pi / 360.0)
    cosine = jnp.cos(angle)[:, None]
    sine = jnp.sin(angle)[:, None]
    radial = picked[0] * cosine + picked[1] * sine
    modelled = jnp.stack([radial, picked[2]], axis=1)
    departure = modelled - arrived[:, 0:2]
    weighted = arrived[:, 2:4] * departure
    back_local = 0.5 * jnp.sum(control * control)
    obs_local = 0.5 * jnp.sum(weighted * departure)
    totals = lax.psum((back_local, obs_local), ("gx", "gy"))
    cost = jnp.stack([totals[0] / (control.size * tiles), totals[1] / (innovation.size * tiles)])
    pushed = jnp.stack([weighted[:, 0] * cosine, weighted[:, 0] * sine, weighted[:, 1]], axis=0)
    adjoint = (
        jnp.zeros((fields, levels * rows_tile, cols_tile), jnp.float32)
        .at[:, row_index, :]
        .add(pushed)
    )
    adjoint = adjoint.reshape(fields, levels, rows_tile, cols_tile) * spread[:, None]
    lifted = jnp.einsum("fkz,fkyx->fzyx", vertical, adjoint, precision=HIGHEST)
    gradient = control + smooth(lifted, east_band, north_band, reach)
    return (gradient, cost)


def solution(mesh):
    placed = (
        P(None, None, "gy", "gx"),
        P(None, "gy", "gx"),
        P(),
        P(),
        P(),
        P(("gx", "gy")),
        P(("gx", "gy")),
        P(("gx", "gy")),
        P(("gx", "gy")),
        P(("gx", "gy"), None, None),
        P(("gx", "gy"), None, None),
    )
    return jax.shard_map(
        body,
        mesh=mesh,
        in_specs=placed,
        out_specs=(P(None, None, "gy", "gx"), P()),
        check_vma=False,
    )
```

profile of v0, /device:TPU:0, one launch (start us, length us, event | category | flops | bytes accessed | tf_op | source)
XLA Modules:
  0.0 499.2 jit_solution(4232596291185757653)
XLA Ops:
  7.9 7.3 %all-to-all-start = ((s32[32,32,3]{1,2,0:T(4,128)}), s32[32,32,3]{1,2,0:T(4,128)S(1)}, u32[]{:S(2)}, u32[]{:S(2)}) async-start(s32[32,32,3]{1,2,0:T(4,128)} %copy.78), calls=%async_computation | async-start | bytes 131072 | tf_op jit(solution)/shard_map/all_to_all | solution.py:46
  18.5 47.5 %scatter_fusion = f32[1024,4,128]{2,1,0:T(4,128)} fusion(f32[1024,4,128]{2,1,0:T(4,128)} %broadcast_in_dim.11, s32[512]{0:T(512)S(1)} %compare_select_fusion.1, f32[512,4,128]{2,1,0:T(4,128)S(1)} %pad_maximum_fusion.1), kind=kCustom, calls=%fused_computation.2 | custom fusion | bytes 3147776 | tf_op jit(solution)/shard_map/scatter | solution.py:74
  66.0 5.8 %all-to-all-start.1 = ((f32[1024,4,128]{2,1,0:T(4,128)}), f32[1024,4,128]{2,1,0:T(4,128)S(1)}, u32[]{:S(2)}, u32[]{:S(2)}) async-start(f32[1024,4,128]{2,1,0:T(4,128)} %scatter_fusion), calls=%async_computation.1 | async-start | bytes 4194304 | tf_op jit(solution)/shard_map/all_to_all | solution.py:45
  71.8 11.2 %fusion.65 = (f32[3,64,64,8]{3,2,1,0:T(8,128)}, f32[3,64,64,8]{3,2,1,0:T(8,128)}) fusion(f32[3,64,64,128]{3,2,1,0:T(8,128)} %param.11), kind=kLoop, calls=%fused_computation.98 | loop fusion | bytes 1572864 | tf_op jit(solution)/shard_map/slice | solution.py:17
  83.0 4.4 copy.118
  87.4 3.1 collective-permute-start
  90.5 5.3 %copy.119 = f32[3,64,64,8]{2,3,1,0:T(8,128)} copy(f32[3,64,64,8]{3,2,1,0:T(8,128)} %get-tuple-element.11) | data formatting | bytes 786432
  98.5 4.9 copy.82
  103.4 4.8 copy.83
  108.2 15.9 %fusion = f32[3,64,64,128]{3,2,1,0:T(8,128)S(1)} fusion(f32[3,64,64,8]{3,2,1,0:T(8,128)} %copy.83, f32[3,64,64,128]{3,2,1,0:T(8,128)} %param.11, f32[3,64,64,8]{3,2,1,0:T(8,128)} %copy.82, f32[3,144,128,1]{2,0,1,3:T(4,128)S(1)} %fusion.33), kind=kOutput, calls=%fused_computation.4 | convolution fusion | flops 2721447936 | bytes 13590528 | tf_op jit(solution)/shard_map/fzyj,fji->fzyi/dot_general | solution.py:38
  128.1 3.6 collective-permute-start.2
  135.1 6.3 %collective-permute-done.2 = f32[3,64,8,128]{3,2,1,0:T(8,128)S(1)} collective-permute-done((f32[3,64,8,128]{3,2,1,0:T(8,128)}, f32[3,64,8,128]{3,2,1,0:T(8,128)S(1)}, u32[]{:S(2)}, u32[]{:S(2)}) %collective-permute-start.2) | collective-permute-done | bytes 786464 | tf_op jit(solution)/shard_map/ppermute | solution.py:16
  141.5 4.4 collective-permute-done.3
  145.9 8.6 %fusion.29 = f32[3,64,64,128]{3,2,1,0:T(8,128)S(1)} fusion(f32[3,64,8,128]{3,2,1,0:T(8,128)} %collective-permute-done.3, f32[3,64,64,128]{3,2,1,0:T(8,128)} %copy-done.3, f32[3,64,8,128]{3,2,1,0:T(8,128)S(1)} %collective-permute-done.2, f32[3,80,64,1]{1,0,2,3:T(4,128)S(1)} %convolution_bitcast_fusion), kind=kOutput, calls=%fused_computation.34 | convolution fusion | flops 1513881600 | bytes 14217216 | tf_op jit(solution)/shard_map/fzjx,fji->fzix/dot_general | solution.py:40
  154.6 10.0 %multiply_bitcast_fusion = f32[3,64,64,128]{3,1,2,0:T(8,128)S(1)} fusion(f32[3,64,128]{2,1,0:T(8,128)S(1)} %copy-done.4, f32[3,64,64,128]{3,2,1,0:T(8,128)S(1)} %fusion.29, f32[3,64,64]{2,1,0:T(8,128)S(1)} %copy-done), kind=kOutput, calls=%fused_computation.31 | convolution fusion | flops 1209532416 | bytes 12730368 | tf_op jit(solution)/shard_map/fkz,fzyx->fkyx/dot_general | solution.py:85
  164.6 4.0 copy.87
  168.6 18.7 %copy.88 = f32[3,4096,128]{2,0,1:T(4,128)} copy(f32[3,4096,128]{2,1,0:T(8,128)S(1)} %bitcast.90) | data formatting | bytes 12582912 | tf_op jit(solution)/shard_map/reshape | solution.py:89
  187.3 11.3 %gather_fusion = f32[1024,3,128]{2,1,0:T(4,128)} fusion(f32[3,4096,128]{2,0,1:T(4,128)} %copy.88, s32[1024]{0:T(1024)S(1)} %broadcast_clamp_fusion), kind=kCustom, calls=%fused_computation | custom fusion | bytes 3149824 | tf_op jit(solution)/shard_map/gather | solution.py:90
  205.3 3.9 broadcast_in_dim.8
  209.1 117.1 %scatter_fusion.1 = f32[3,4096,128]{2,0,1:T(4,128)} fusion(f32[3,4096,128]{2,0,1:T(4,128)} %broadcast_in_dim.8, s32[1024]{0:T(1024)S(1)} %bitcast.103, f32[1024,3,128]{2,1,0:T(4,128)S(1)} %copy.92), kind=kCustom, calls=%fused_computation.3 | custom fusion | flops 393216 | bytes 4722688 | tf_op jit(solution)/shard_map/scatter-add | solution.py:106
  326.2 12.9 %fusion.26 = f32[3,64,64,128]{3,1,2,0:T(8,128)S(1)} fusion(f32[3,64,64,128]{3,0,2,1:T(4,128)} %bitcast.89, f32[3,64,128]{2,1,0:T(8,128)} %param.12, f32[3,64,64]{2,1,0:T(8,128)S(1)} %copy-done), kind=kOutput, calls=%fused_computation.33 | convolution fusion | flops 1209532416 | bytes 12730368 | tf_op jit(solution)/shard_map/fkz,fkyx->fzyx/dot_general | solution.py:109
  339.1 6.7 %fusion.63 = (f32[3,64,64,8]{3,1,2,0:T(8,128)}, f32[3,64,64,8]{3,1,2,0:T(8,128)}) fusion(f32[3,64,64,128]{3,1,2,0:T(8,128)S(1)} %fusion.26), kind=kLoop, calls=%fused_computation.96 | loop fusion | bytes 1572864 | tf_op jit(solution)/shard_map/slice | solution.py:17
  345.8 5.2 %copy.95 = f32[3,64,64,8]{2,3,1,0:T(8,128)S(1)} copy(f32[3,64,64,8]{3,1,2,0:T(8,128)} %get-tuple-element.6) | data formatting | bytes 786432 | tf_op jit(solution)/shard_map/slice | solution.py:17
  351.0 17.2 %collective-permute-start.4 = (f32[3,64,64,8]{2,3,1,0:T(8,128)S(1)}, f32[3,64,64,8]{2,3,1,0:T(8,128)S(1)}, u32[]{:S(2)}, u32[]{:S(2)}) collective-permute-start(f32[3,64,64,8]{2,3,1,0:T(8,128)S(1)} %copy.95), channel_id=1, source_target_pairs={{0,4},{4,8},{8,12},{12,16},{16,20},{20,24},{24,28},{1,5},{5,9},{9,... | collective-permute-start | bytes 1179656 | tf_op jit(solution)/shard_map/ppermute | solution.py:16
  368.2 5.2 %copy.96 = f32[3,64,64,8]{2,3,1,0:T(8,128)S(1)} copy(f32[3,64,64,8]{3,1,2,0:T(8,128)} %get-tuple-element.7) | data formatting | bytes 786432 | tf_op jit(solution)/shard_map/slice | solution.py:19
  374.7 5.9 %copy.97 = f32[3,64,64,8]{3,1,2,0:T(8,128)} copy(f32[3,64,64,8]{2,3,1,0:T(8,128)S(1)} %collective-permute-done.4) | data formatting | bytes 786432 | tf_op jit(solution)/shard_map/ppermute | solution.py:16
  380.6 2.7 collective-permute-done.5
  383.4 5.9 %copy.98 = f32[3,64,64,8]{3,1,2,0:T(8,128)} copy(f32[3,64,64,8]{2,3,1,0:T(8,128)S(1)} %collective-permute-done.5) | data formatting | bytes 786432 | tf_op jit(solution)/shard_map/ppermute | solution.py:19
  389.3 10.2 %pad_maximum_fusion = f32[3,64,64,144]{3,1,2,0:T(8,128)S(1)} fusion(f32[3,64,64,8]{3,1,2,0:T(8,128)} %copy.98, f32[3,64,64,128]{3,1,2,0:T(8,128)} %copy-done.1, f32[3,64,64,8]{3,1,2,0:T(8,128)} %copy.97), kind=kLoop, calls=%fused_computation.10 | loop fusion | flops 3538944 | bytes 14155776 | tf_op jit(solution)/shard_map/concatenate | solution.py:20
  399.5 18.6 %fusion.6 = f32[3,64,64,128]{3,2,1,0:T(8,128)S(1)} fusion(f32[3,64,64,144]{3,1,2,0:T(8,128)S(1)} %pad_maximum_fusion, f32[3,144,128,1]{2,0,1,3:T(4,128)S(1)} %fusion.33), kind=kOutput, calls=%fused_computation.11 | convolution fusion | flops 2717908992 | bytes 13590528 | tf_op jit(solution)/shard_map/fzyj,fji->fzyi/dot_general | solution.py:38
  428.2 58.9 %all-reduce = (f32[]{:T(128)}, f32[]{:T(128)}) all-reduce(f32[]{:T(128)S(6)} %mul.142, f32[]{:T(128)S(6)} %mul.140), channel_id=1, replica_groups=mesh['gx'=8,'gy'=4] {'gx','gy'}, use_global_device_ids=true, to_apply=%region_9.10 | all-reduce | flops 2 | bytes 16 | tf_op jit(solution)/shard_map/psum | solution.py:100
  488.9 10.1 %bitcast_add_fusion = f32[3,64,64,128]{3,2,1,0:T(8,128)} fusion(f32[3,64,64,128]{3,2,1,0:T(8,128)} %param.11, f32[3,64,8,128]{3,2,1,0:T(8,128)} %collective-permute-done.7, f32[3,64,64,128]{3,2,1,0:T(8,128)} %copy-done.2, f32[3,64,8,128]{3,2,1,0:T(8,128)S(1)} %collective-permute-done.6, f32[3,80,64,1]{1,0,2,3:T(4,128)S(1)} %copy-done.6), kind=kOutput, calls=%fused_computation.25 | convolution fusion | flops 1515454464 | bytes 20508672 | tf_op jit(solution)/shard_map/fzjx,fji->fzix/dot_general | solution.py:40
  (73 shorter events, 38.1 us)
Async XLA Ops:
  0.6 153.9 %copy-start = (f32[3,64,64]{2,1,0:T(8,128)S(1)}, f32[3,64,64]{2,1,0:T(8,128)}, u32[]{:S(2)}) copy-start(f32[3,64,64]{2,1,0:T(8,128)} %param.15) | copy-start | bytes 147460
  7.9 58.1 %all-to-all-start = ((s32[32,32,3]{1,2,0:T(4,128)}), s32[32,32,3]{1,2,0:T(4,128)S(1)}, u32[]{:S(2)}, u32[]{:S(2)}) async-start(s32[32,32,3]{1,2,0:T(4,128)} %copy.78), calls=%async_computation | async-start | bytes 131072 | tf_op jit(solution)/shard_map/all_to_all | solution.py:46
  66.0 134.6 %all-to-all-start.1 = ((f32[1024,4,128]{2,1,0:T(4,128)}), f32[1024,4,128]{2,1,0:T(4,128)S(1)}, u32[]{:S(2)}, u32[]{:S(2)}) async-start(f32[1024,4,128]{2,1,0:T(4,128)} %scatter_fusion), calls=%async_computation.1 | async-start | bytes 4194304 | tf_op jit(solution)/shard_map/all_to_all | solution.py:45
  83.0 14.5 %copy-start.7 = (f32[3,9]{1,0:T(4,128)S(1)}, f32[3,9]{1,0:T(4,128)}, u32[]{:S(2)}) copy-start(f32[3,9]{1,0:T(4,128)} %param.13) | copy-start | bytes 328
  83.0 14.6 %copy-start.8 = (f32[3,9]{1,0:T(4,128)S(1)}, f32[3,9]{1,0:T(4,128)}, u32[]{:S(2)}) copy-start(f32[3,9]{1,0:T(4,128)} %param.14) | copy-start | bytes 328
  87.4 11.1 %collective-permute-start = (f32[3,64,64,8]{2,3,1,0:T(8,128)S(1)}, f32[3,64,64,8]{2,3,1,0:T(8,128)}, u32[]{:S(2)}, u32[]{:S(2)}) collective-permute-start(f32[3,64,64,8]{2,3,1,0:T(8,128)S(1)} %copy.118), channel_id=1, source_target_pairs={{0,4},{4,8},{8,12},{12,16},{16,20},{20,24},{24,28},{1,5},{5,9},{9,... | collective-permute-start | bytes 1179656 | tf_op jit(solution)/shard_map/ppermute | solution.py:16
  95.7 7.7 %collective-permute-start.1 = (f32[3,64,64,8]{2,3,1,0:T(8,128)}, f32[3,64,64,8]{2,3,1,0:T(8,128)}, u32[]{:S(2)}, u32[]{:S(2)}) collective-permute-start(f32[3,64,64,8]{2,3,1,0:T(8,128)} %copy.119), channel_id=1, source_target_pairs={{4,0},{8,4},{12,8},{16,12},{20,16},{24,20},{28,24},{5,1},{9,5},{13... | collective-permute-start | bytes 1179656 | tf_op jit(solution)/shard_map/ppermute | solution.py:19
  124.1 2.7 copy-start.3
  128.1 13.4 %collective-permute-start.2 = (f32[3,64,8,128]{3,2,1,0:T(8,128)}, f32[3,64,8,128]{3,2,1,0:T(8,128)S(1)}, u32[]{:S(2)}, u32[]{:S(2)}) collective-permute-start(f32[3,64,8,128]{3,2,1,0:T(8,128)} %get-tuple-element.8), channel_id=1, source_target_pairs={{0,1},{1,2},{2,3},{4,5},{5,6},{6,7},{8,9},{9,10},{10,11},{12,13},{... | collective-permute-start | bytes 2359304 | tf_op jit(solution)/shard_map/ppermute | solution.py:16
  131.7 14.2 %collective-permute-start.3 = (f32[3,64,8,128]{3,2,1,0:T(8,128)}, f32[3,64,8,128]{3,2,1,0:T(8,128)}, u32[]{:S(2)}, u32[]{:S(2)}) collective-permute-start(f32[3,64,8,128]{3,2,1,0:T(8,128)} %get-tuple-element.9), channel_id=1, source_target_pairs={{1,0},{2,1},{3,2},{5,4},{6,5},{7,6},{9,8},{10,9},{11,10},{13,12},{... | collective-permute-start | bytes 2359304 | tf_op jit(solution)/shard_map/ppermute | solution.py:19
  133.4 21.2 %copy-start.5 = (f32[3,80,64,1]{1,0,2,3:T(4,128)}, f32[3,80,64,1]{1,0,2,3:T(4,128)S(1)}, u32[]{:S(2)}) copy-start(f32[3,80,64,1]{1,0,2,3:T(4,128)S(1)} %convolution_bitcast_fusion) | copy-start | bytes 184324
  135.1 19.5 %copy-start.4 = (f32[3,64,128]{2,1,0:T(8,128)S(1)}, f32[3,64,128]{2,1,0:T(8,128)}, u32[]{:S(2)}) copy-start(f32[3,64,128]{2,1,0:T(8,128)} %param.12) | copy-start | bytes 294916
  339.1 6.7 %copy-start.1 = (f32[3,64,64,128]{3,1,2,0:T(8,128)}, f32[3,64,64,128]{3,1,2,0:T(8,128)S(1)}, u32[]{:S(2)}) copy-start(f32[3,64,64,128]{3,1,2,0:T(8,128)S(1)} %fusion.26) | copy-start | bytes 18874372
  351.0 23.7 %collective-permute-start.4 = (f32[3,64,64,8]{2,3,1,0:T(8,128)S(1)}, f32[3,64,64,8]{2,3,1,0:T(8,128)S(1)}, u32[]{:S(2)}, u32[]{:S(2)}) collective-permute-start(f32[3,64,64,8]{2,3,1,0:T(8,128)S(1)} %copy.95), channel_id=1, source_target_pairs={{0,4},{4,8},{8,12},{12,16},{16,20},{20,24},{24,28},{1,5},{5,9},{9,... | collective-permute-start | bytes 1179656 | tf_op jit(solution)/shard_map/ppermute | solution.py:16
  373.4 9.9 %collective-permute-start.5 = (f32[3,64,64,8]{2,3,1,0:T(8,128)S(1)}, f32[3,64,64,8]{2,3,1,0:T(8,128)S(1)}, u32[]{:S(2)}, u32[]{:S(2)}) collective-permute-start(f32[3,64,64,8]{2,3,1,0:T(8,128)S(1)} %copy.96), channel_id=1, source_target_pairs={{4,0},{8,4},{12,8},{16,12},{20,16},{24,20},{28,24},{5,1},{9,5},{13... | collective-permute-start | bytes 1179656 | tf_op jit(solution)/shard_map/ppermute | solution.py:19
  383.4 41.3 %slice-start = ((s8[6291456]{0:T(1024)(128)(4,1)}), s8[2097152]{0:T(1024)(128)(4,1)S(1)}, s32[]{:S(2)}) async-start(s8[6291456]{0:T(1024)(128)(4,1)} %bitcast.87), calls=%async_computation.2 | async-start | bytes 4194304
  389.3 35.4 %slice-start.1 = ((s8[6291456]{0:T(1024)(128)(4,1)}), s8[4194304]{0:T(1024)(128)(4,1)S(1)}, s32[]{:S(2)}) async-start(s8[6291456]{0:T(1024)(128)(4,1)} %bitcast.87), calls=%async_computation.3 | async-start | bytes 8388608
  418.0 2.7 copy-start.2
  420.7 68.2 %copy-start.6 = (f32[3,80,64,1]{1,0,2,3:T(4,128)S(1)}, f32[3,80,64,1]{1,0,2,3:T(4,128)}, u32[]{:S(2)}) copy-start(f32[3,80,64,1]{1,0,2,3:T(4,128)} %copy-done.5) | copy-start | bytes 184324
  422.0 67.0 %collective-permute-start.6 = (f32[3,64,8,128]{3,2,1,0:T(8,128)}, f32[3,64,8,128]{3,2,1,0:T(8,128)S(1)}, u32[]{:S(2)}, u32[]{:S(2)}) collective-permute-start(f32[3,64,8,128]{3,2,1,0:T(8,128)} %get-tuple-element.4), channel_id=1, source_target_pairs={{0,1},{1,2},{2,3},{4,5},{5,6},{6,7},{8,9},{9,10},{10,11},{12,13},{... | collective-permute-start | bytes 2359304 | tf_op jit(solution)/shard_map/ppermute | solution.py:16
  423.3 65.6 %collective-permute-start.7 = (f32[3,64,8,128]{3,2,1,0:T(8,128)}, f32[3,64,8,128]{3,2,1,0:T(8,128)}, u32[]{:S(2)}, u32[]{:S(2)}) collective-permute-start(f32[3,64,8,128]{3,2,1,0:T(8,128)} %get-tuple-element.5), channel_id=1, source_target_pairs={{1,0},{2,1},{3,2},{5,4},{6,5},{7,6},{9,8},{10,9},{11,10},{13,12},{... | collective-permute-start | bytes 2359304 | tf_op jit(solution)/shard_map/ppermute | solution.py:19
where the time goes:
time: 509 us; the launch traced here: 499 us
  local copies, waits for them, and re-layouts  163 us (32%)
  other arithmetic  139 us (27%)
  matrix products  77 us (15%)
  blocking collectives  58.9 us (12%)
  starting transfers between devices  43.9 us (9%)
  waiting for transfers between devices  13.5 us (3%)
    scatter-add x1, other arithmetic, body(): adjoint = jnp.zeros((fields, levels * rows_tile, cols_tile), jnp.float32)...  117 us
    psum x1, blocking collectives, body(): totals = lax.psum((back_local, obs_local), ('gx', 'gy'))  58.9 us
    scatter x1, local copies, waits for them, and re-layouts, body(): payload = jnp.zeros((tiles * most, 4, cols_tile), jnp.float32).at[slot].s...  47.5 us
    dot_general x2, matrix products, smooth(): jnp.einsum('fzyj,fji->fzyi', widened, east_band, precision=HIGHEST)  34.4 us
    slice x5, local copies, waits for them, and re-layouts, padded(): lax.slice_in_dim(block, block.shape[dim] - width, None, axis=dim)  25.7 us
    ppermute x4, starting transfers between devices, padded(): lax.ppermute(lax.slice_in_dim(block, block.shape[dim] - width, None, axis...  25.2 us
    dot_general x2, matrix products, smooth(): return jnp.einsum('fzjx,fji->fzix', across, north_band, precision=HIGHEST)  18.7 us
    reshape x1, local copies, waits for them, and re-layouts, body(): flat_state = state_field.reshape(fields, levels * rows_tile, cols_tile)  18.7 us
  transfers between devices with their start and end apart: 10, of which 3 were waited for; matrix products, arithmetic and copies ran while one was open for 34% of the time, Pallas kernels for 0%

commit v1 on v0

v1 whole, which is shorter than its diff:
```python
import functools
import math

import jax
import jax.numpy as jnp
from jax import lax
from jax.experimental import pallas as pl
from jax.experimental.pallas import tpu as pltpu
from jax.sharding import PartitionSpec as P

F32 = jnp.float32
BF16 = jnp.bfloat16
VMEM_BYTES = 56 * 1024 * 1024


def params():
    return pltpu.CompilerParams(vmem_limit_bytes=VMEM_BYTES)


def split(value):
    high = value.astype(BF16)
    low = (value - high.astype(F32)).astype(BF16)
    return high, low


def doubled(weights):
    high, low = split(weights)
    row = jnp.concatenate([high, low], axis=1)
    return jnp.concatenate([row, row], axis=0)


def times(rows, weights):
    high, low = split(rows)
    both = jnp.dot(
        jnp.concatenate([high, low], axis=1), weights, preferred_element_type=F32
    )
    half = both.shape[1] // 2
    return both[:, :half] + both[:, half:]


def taps_at(kernel_ref, f, distance, allowed):
    total = jnp.zeros(distance.shape, F32)
    for d in range(kernel_ref.shape[1]):
        total = jnp.where(distance == d, kernel_ref[f, d], total)
    return jnp.where(allowed, total, 0.0)


def main_band(kernel_ref, f):
    r = lax.broadcasted_iota(jnp.int32, (128, 128), 0)
    c = lax.broadcasted_iota(jnp.int32, (128, 128), 1)
    return doubled(taps_at(kernel_ref, f, jnp.abs(r - c), jnp.abs(r - c) <= 8))


def rim_band(kernel_ref, f, offset):
    r = (lax.broadcasted_iota(jnp.int32, (128, 128), 0) + (128 - offset)) & 127
    c = (lax.broadcasted_iota(jnp.int32, (128, 128), 1) + (128 - offset)) & 127
    distance = jnp.abs(r - c)
    fits = ((r >> 4) == (c >> 4)) & ((r & 8) != (c & 8)) & (distance <= 8)
    return doubled(taps_at(kernel_ref, f, distance, fits))


def pack_rims(get, put_right, put_left, groups, b):
    lane = lax.broadcasted_iota(jnp.int32, (b, 128), 1)
    first = (lane & 8) == 0

    def one(g, carry):
        even = jnp.zeros((b, 128), F32)
        odd = jnp.zeros((b, 128), F32)
        for q in range(8):
            even = jnp.where(
                (lane >> 4) == q, pltpu.roll(get(16 * g + 2 * q), (16 * q + 8) % 128, 1), even
            )
            odd = jnp.where(
                (((lane + 120) & 127) >> 4) == q,
                pltpu.roll(get(16 * g + 2 * q + 1), (16 * q + 16) % 128, 1),
                odd,
            )
        put_right(g, jnp.where(first, even, odd))
        put_left(g, jnp.where(first, odd, even))
        return carry

    lax.fori_loop(0, groups, one, 0)


def east_filter(get, low_ref, high_ref, put, kernel_ref, f, groups, b):
    band = main_band(kernel_ref, f)
    rim_even = rim_band(kernel_ref, f, 0)
    rim_odd = rim_band(kernel_ref, f, 8)
    lane = lax.broadcasted_iota(jnp.int32, (b, 128), 1)
    first = (lane & 8) == 0
    edge = (lane < 8) | (lane >= 120)

    def one(g, carry):
        low = low_ref[0, g]
        high = high_ref[0, g]
        even = times(jnp.where(first, low, high), rim_even)
        odd = times(jnp.where(first, high, low), rim_odd)
        for q in range(8):
            a = 16 * g + 2 * q
            pair = jnp.concatenate([get(a), get(a + 1)], axis=0)
            flat = times(pair, band)
            put(a, flat[:b] + jnp.where(edge, pltpu.roll(even, (248 - 16 * q) % 128, 1), 0.0))
            put(a + 1, flat[b:] + jnp.where(edge, pltpu.roll(odd, (240 - 16 * q) % 128, 1), 0.0))
        return carry

    lax.fori_loop(0, groups, one, 0)


def north_filter(slab_ref, kernel_ref, f, y0, kb):
    u = slab_ref[pl.ds(y0, 24), pl.ds(kb, 8), :]
    total = kernel_ref[f, 0] * u[8:16]
    for d in range(1, 9):
        total = total + kernel_ref[f, d] * (u[8 - d : 16 - d] + u[8 + d : 16 + d])
    return total


def fold_rows(x):
    return jnp.sum(x.reshape(-1, 8, 128), axis=0)


def rows_kernel(most, owner, level, row, azimuth, inn, wt, out, labels, count):
    rows = owner.shape[0]
    tiles = count.shape[0]
    out[...] = jnp.zeros_like(out)

    def clear(t, carry):
        count[t] = 0
        for j in range(3 * most):
            labels[t * 3 * most + j] = 0
        return carry

    lax.fori_loop(0, tiles, clear, 0)

    def one(i, carry):
        for j in range(4):
            r = i * 4 + j
            o = owner[r]
            rank = count[o]
            count[o] = rank + 1
            at = o * (3 * most) + rank
            labels[at] = level[r]
            labels[at + most] = row[r]
            labels[at + 2 * most] = azimuth[r]
            slot = o * most + rank
            out[slot, 0:2] = inn[r]
            out[slot, 2:4] = wt[r]
        return carry

    lax.fori_loop(0, rows // 4, one, 0)


def pack_rows(owner, level, row, azimuth, inn, wt, tiles, most):
    smem = pl.BlockSpec(memory_space=pltpu.SMEM)
    vmem = pl.BlockSpec(memory_space=pltpu.VMEM)
    return pl.pallas_call(
        functools.partial(rows_kernel, most),
        out_shape=(
            jax.ShapeDtypeStruct((tiles * most, 4, 128), F32),
            jax.ShapeDtypeStruct((tiles * 3 * most,), jnp.int32),
        ),
        in_specs=[smem] * 4 + [vmem] * 2,
        out_specs=(vmem, smem),
        scratch_shapes=[pltpu.SMEM((tiles,), jnp.int32)],
        compiler_params=params(),
        name="pack_rows",
    )(owner, level, row, azimuth, inn, wt)


def rims_kernel(c_ref, right, left, square):
    a, b = c_ref.shape[1], c_ref.shape[2]

    def put_right(g, v):
        right[0, g] = v

    def put_left(g, v):
        left[0, g] = v

    pack_rims(lambda s: c_ref[0, s], put_right, put_left, a // 16, b)

    def one(s, total):
        v = c_ref[0, s]
        return total + fold_rows(v * v)

    square[0] = lax.fori_loop(0, a, one, jnp.zeros((8, 128), F32))


def control_rims(control):
    f, a, b, w = control.shape
    rim = pl.BlockSpec((1, a // 16, b, w), lambda i: (i, 0, 0, 0))
    rim_shape = jax.ShapeDtypeStruct((f, a // 16, b, w), F32)
    return pl.pallas_call(
        rims_kernel,
        grid=(f,),
        in_specs=[pl.BlockSpec((1, a, b, w), lambda i: (i, 0, 0, 0))],
        out_specs=(rim, rim, pl.BlockSpec((1, 8, w), lambda i: (i, 0, 0))),
        out_shape=(rim_shape, rim_shape, jax.ShapeDtypeStruct((f, 8, w), F32)),
        compiler_params=params(),
        name="control_rims",
    )(control)


def forward_kernel(c_ref, low, high, vert, kernel_ref, out, top, bottom, flat):
    f = pl.program_id(0)
    a, b = c_ref.shape[1], c_ref.shape[2]

    def put(s, v):
        flat[pl.ds(pl.multiple_of(s * b, b), b), :] = v

    east_filter(lambda s: c_ref[0, s], low, high, put, kernel_ref, f, a // 16, b)
    v = vert[0]

    def one(p, carry):
        for j in range(4):
            y = p * 8 + 2 * j
            x = jnp.concatenate(
                [flat[pl.ds(y, a, stride=b), :], flat[pl.ds(y + 1, a, stride=b), :]], axis=1
            )
            h, l = split(x)
            r = jnp.dot(v, jnp.concatenate([h, l, h, l], axis=0), preferred_element_type=F32)
            out[0, y] = r[:, :128]
            out[0, y + 1] = r[:, 128:]
        return carry

    lax.fori_loop(0, b // 8, one, 0)
    top[0] = out[0, b - 8 :]
    bottom[0] = out[0, :8]


def forward(control, low, high, vert, kernel_east):
    f, a, b, w = control.shape
    rim = pl.BlockSpec((1, a // 16, b, w), lambda i: (i, 0, 0, 0))
    edge = pl.BlockSpec((1, 8, a, w), lambda i: (i, 0, 0, 0))
    edge_shape = jax.ShapeDtypeStruct((f, 8, a, w), F32)
    return pl.pallas_call(
        forward_kernel,
        grid=(f,),
        in_specs=[
            pl.BlockSpec((1, a, b, w), lambda i: (i, 0, 0, 0)),
            rim,
            rim,
            pl.BlockSpec((1, a, 4 * a), lambda i: (i, 0, 0)),
            pl.BlockSpec(memory_space=pltpu.SMEM),
        ],
        out_specs=(pl.BlockSpec((1, b, a, w), lambda i: (i, 0, 0, 0)), edge, edge),
        out_shape=(jax.ShapeDtypeStruct((f, b, a, w), F32), edge_shape, edge_shape),
        scratch_shapes=[pltpu.VMEM((a * b, w), F32)],
        compiler_params=params(),
        name="forward",
    )(control, low, high, vert, kernel_east)


def observe_kernel(
    cell, cosine, sine, kernel_ref, u_ref, low, high, spread, rows_ref,
    adj, right, left, obs,
    slab, s0, s1, s2, a0, a1, a2, m0, m1,
):
    fields, b, a, w = u_ref.shape
    states = (s0, s1, s2)
    adjs = (a0, a1, a2)
    for f in range(fields):
        slab[0:8] = low[f]
        slab[8 : 8 + b] = u_ref[f]
        slab[8 + b :] = high[f]
        state = states[f]
        grown = adjs[f]

        def one(i, carry):
            y0 = (i // (a // 8)) * 8
            kb = pl.multiple_of((i % (a // 8)) * 8, 8)
            total = north_filter(slab, kernel_ref, f, y0, kb)
            for j in range(8):
                scale = spread[f, pl.ds(y0 + j, 1), :]
                at = pl.multiple_of((y0 + j) * a + kb, 8)
                state[pl.ds(at, 8), :] = total[j] * scale
                grown[pl.ds(at, 8), :] = jnp.zeros((8, w), F32)
            return carry

        lax.fori_loop(0, (b // 8) * (a // 8), one, 0)

    count = rows_ref.shape[0]

    def pick(i, carry):
        for j in range(8):
            r = i * 8 + j
            at = cell[r]
            m0[pl.ds(r, 1), :] = cosine[r] * s0[pl.ds(at, 1), :] + sine[r] * s1[pl.ds(at, 1), :]
            m1[pl.ds(r, 1), :] = s2[pl.ds(at, 1), :]
        return carry

    lax.fori_loop(0, count // 8, pick, 0)

    def weigh(i, total):
        at = pl.ds(pl.multiple_of(i * 8, 8), 8)
        d0 = m0[at, :] - rows_ref[at, 0, :]
        d1 = m1[at, :] - rows_ref[at, 1, :]
        w0 = rows_ref[at, 2, :] * d0
        w1 = rows_ref[at, 3, :] * d1
        m0[at, :] = w0
        m1[at, :] = w1
        return total + (w0 * d0 + w1 * d1)

    obs[...] = lax.fori_loop(0, count // 8, weigh, jnp.zeros((8, w), F32))

    def push(i, carry):
        for j in range(8):
            r = i * 8 + j
            at = pl.ds(cell[r], 1)
            w0 = m0[pl.ds(r, 1), :]
            a0[at, :] = a0[at, :] + cosine[r] * w0
            a1[at, :] = a1[at, :] + sine[r] * w0
            a2[at, :] = a2[at, :] + m1[pl.ds(r, 1), :]
        return carry

    lax.fori_loop(0, count // 8, push, 0)
    for f in range(fields):
        grown = adjs[f]

        def scale_rows(y, carry):
            at = pl.ds(pl.multiple_of(y * a, a), a)
            adj[f, y] = grown[at, :] * spread[f, pl.ds(y, 1), :]
            return carry

        lax.fori_loop(0, b, scale_rows, 0)

        def put_right(g, v):
            right[f, g] = v

        def put_left(g, v):
            left[f, g] = v

        pack_rims(lambda s: adj[f, s], put_right, put_left, b // 16, a)


def observe(cell, cosine, sine, kernel_north, u, low, high, spread, rows):
    f, b, a, w = u.shape
    smem = pl.BlockSpec(memory_space=pltpu.SMEM)
    vmem = pl.BlockSpec(memory_space=pltpu.VMEM)
    rim = jax.ShapeDtypeStruct((f, b // 16, a, w), F32)
    return pl.pallas_call(
        observe_kernel,
        in_specs=[smem] * 4 + [vmem] * 5,
        out_specs=(vmem,) * 4,
        out_shape=(
            jax.ShapeDtypeStruct((f, b, a, w), F32),
            rim,
            rim,
            jax.ShapeDtypeStruct((8, w), F32),
        ),
        scratch_shapes=[pltpu.VMEM((b + 16, a, w), F32)]
        + [pltpu.VMEM((a * b, w), F32)] * 6
        + [pltpu.VMEM((rows.shape[0], w), F32)] * 2,
        compiler_params=params(),
        name="observe",
    )(cell, cosine, sine, kernel_north, u, low, high, spread, rows)


def back_east_kernel(x_ref, low, high, kernel_ref, out, top, bottom):
    f = pl.program_id(0)
    b, a = x_ref.shape[1], x_ref.shape[2]

    def put(s, v):
        out[0, s] = v

    east_filter(lambda s: x_ref[0, s], low, high, put, kernel_ref, f, b // 16, a)
    top[0] = out[0, b - 8 :]
    bottom[0] = out[0, :8]


def back_east(x, low, high, kernel_east):
    f, b, a, w = x.shape
    rim = pl.BlockSpec((1, b // 16, a, w), lambda i: (i, 0, 0, 0))
    edge = pl.BlockSpec((1, 8, a, w), lambda i: (i, 0, 0, 0))
    edge_shape = jax.ShapeDtypeStruct((f, 8, a, w), F32)
    full = pl.BlockSpec((1, b, a, w), lambda i: (i, 0, 0, 0))
    return pl.pallas_call(
        back_east_kernel,
        grid=(f,),
        in_specs=[full, rim, rim, pl.BlockSpec(memory_space=pltpu.SMEM)],
        out_specs=(full, edge, edge),
        out_shape=(jax.ShapeDtypeStruct((f, b, a, w), F32), edge_shape, edge_shape),
        compiler_params=params(),
        name="back_east",
    )(x, low, high, kernel_east)


def gradient_kernel(x_ref, low, high, vert, kernel_ref, c_ref, out, slab, flat):
    f = pl.program_id(0)
    b, a, w = x_ref.shape[1:]
    slab[0:8] = low[0]
    slab[8 : 8 + b] = x_ref[0]
    slab[8 + b :] = high[0]

    def one(i, carry):
        y0 = (i // (a // 8)) * 8
        kb = pl.multiple_of((i % (a // 8)) * 8, 8)
        total = north_filter(slab, kernel_ref, f, y0, kb)
        for j in range(8):
            flat[y0 + j, pl.ds(kb, 8), :] = total[j]
        return carry

    lax.fori_loop(0, (b // 8) * (a // 8), one, 0)
    v = vert[0]

    def two(p, carry):
        for j in range(4):
            y = p * 8 + 2 * j
            x = jnp.concatenate([flat[y], flat[y + 1]], axis=1)
            h, l = split(x)
            r = jnp.dot(v, jnp.concatenate([h, l, h, l], axis=0), preferred_element_type=F32)
            s0 = pl.ds(y, a, stride=b)
            s1 = pl.ds(y + 1, a, stride=b)
            out[0, s0, :] = c_ref[0, s0, :] + r[:, :128]
            out[0, s1, :] = c_ref[0, s1, :] + r[:, 128:]
        return carry

    lax.fori_loop(0, b // 8, two, 0)


def gradient_of(x, low, high, vert, kernel_north, control):
    f, b, a, w = x.shape
    edge = pl.BlockSpec((1, 8, a, w), lambda i: (i, 0, 0, 0))
    flat = pl.BlockSpec((1, a * b, w), lambda i: (i, 0, 0))
    return pl.pallas_call(
        gradient_kernel,
        grid=(f,),
        in_specs=[
            pl.BlockSpec((1, b, a, w), lambda i: (i, 0, 0, 0)),
            edge,
            edge,
            pl.BlockSpec((1, a, 4 * a), lambda i: (i, 0, 0)),
            pl.BlockSpec(memory_space=pltpu.SMEM),
            flat,
        ],
        out_specs=flat,
        out_shape=jax.ShapeDtypeStruct((f, a * b, w), F32),
        scratch_shapes=[pltpu.VMEM((b + 16, a, w), F32), pltpu.VMEM((b, a, w), F32)],
        compiler_params=params(),
        name="gradient",
    )(x, low, high, vert, kernel_north, control.reshape(f, a * b, w)).reshape(control.shape)


def exchange(up, down, axis):
    count = lax.axis_size(axis)
    forward_pairs = [(i, i + 1) for i in range(count - 1)]
    backward = [(t, s) for s, t in forward_pairs]
    return lax.ppermute(up, axis, forward_pairs), lax.ppermute(down, axis, backward)


def vertical_parts(v):
    high = lax.reduce_precision(v, 8, 7)
    low = lax.reduce_precision(v - high, 8, 7)
    return jnp.concatenate([high, high, low, low], axis=2).astype(BF16)


def body(
    control, spread, kernel_east, kernel_north, vertical,
    tile_owner, gate_level, tile_row, beam_azimuth, innovation, obs_weight,
):
    tiles = lax.axis_size("gx") * lax.axis_size("gy")
    most = 2 * tile_owner.shape[0] // tiles
    levels = control.shape[1]
    axes = ("gx", "gy")

    right, left, square = control_rims(control)
    low, high = exchange(right, left, "gx")
    rows, labels = pack_rows(
        tile_owner, gate_level, tile_row, beam_azimuth, innovation, obs_weight, tiles, most
    )
    rows = lax.all_to_all(rows, axes, split_axis=0, concat_axis=0, tiled=True)
    labels = lax.all_to_all(
        labels.reshape(tiles, 3, most), axes, split_axis=0, concat_axis=0, tiled=True
    )
    vert = vertical_parts(vertical)
    vert_back = vertical_parts(jnp.swapaxes(vertical, 1, 2))
    u, top, bottom = forward(control, low, high, vert, kernel_east)
    south, north = exchange(top, bottom, "gy")
    cell = (labels[:, 1] * levels + labels[:, 0]).reshape(-1)
    angle = labels[:, 2].reshape(-1).astype(F32) * (2.0 * math.pi / 360.0)
    adj, right, left, obs = observe(
        cell, jnp.cos(angle), jnp.sin(angle), kernel_north, u, south, north, spread, rows
    )
    parts = jnp.stack([jnp.sum(square), jnp.sum(obs)])
    totals = jnp.sum(lax.all_gather(parts, axes), axis=0)
    counts = jnp.array([control.size * tiles, innovation.size * tiles], F32)
    cost = 0.5 * totals / counts
    low, high = exchange(right, left, "gx")
    g, top, bottom = back_east(adj, low, high, kernel_east)
    south, north = exchange(top, bottom, "gy")
    gradient = gradient_of(g, south, north, vert_back, kernel_north, control)
    return gradient, cost


def solution(mesh):
    both = ("gx", "gy")
    placed = (
        P(None, None, "gy", "gx"),
        P(None, "gy", "gx"),
        P(),
        P(),
        P(),
        P(both),
        P(both),
        P(both),
        P(both),
        P(both, None, None),
        P(both, None, None),
    )
    return jax.shard_map(
        body,
        mesh=mesh,
        in_specs=placed,
        out_specs=(P(None, None, "gy", "gx"), P()),
        check_vma=False,
    )
```

time: 509 us -> 226 us (0.44); the launches traced: 499 us -> 225 us
  local copies, waits for them, and re-layouts: 163 us -> 6.96 us
  other arithmetic: 139 us -> 5.35 us
  Pallas kernels: 0 us -> 94.7 us
  matrix products: 77 us -> 0 us
  starting transfers between devices: 43.9 us -> 28.2 us
  waiting for transfers between devices: 13.5 us -> 27.7 us
    scatter-add x1 -> x0, other arithmetic: 117 us -> none  [body(): adjoint = jnp.zeros((fields, levels * rows_tile, cols_tile), jnp.float32)...]
    pallas_call x0 -> x6, Pallas kernels: none -> 94.7 us  [the longest x1 30.9 us: observe(): pl.pallas_call(observe_kernel, in_specs=[smem] * 4 + [vmem] * 5, out_spec...]
    dot_general x8 -> x0, matrix products: 77 us -> none  [the longest x2 34.4 us: smooth(): jnp.einsum('fzyj,fji->fzyi', widened, east_band, precision=HIGHEST)]
    psum x1 -> x0, blocking collectives: 58.9 us -> none  [body(): totals = lax.psum((back_local, obs_local), ('gx', 'gy'))]
    scatter x2 -> x0, local copies, waits for them, and re-layouts: 49.3 us -> none  [the longest x1 47.5 us: body(): payload = jnp.zeros((tiles * most, 4, cols_tile), jnp.float32).at[slot].s...]
    unnamed x0 -> x1, blocking collectives: none -> 47 us
    slice x11 -> x0, local copies, waits for them, and re-layouts: 32.1 us -> none  [the longest x5 25.7 us: padded(): lax.slice_in_dim(block, block.shape[dim] - width, None, axis=dim)]
    ppermute x4 -> x0, local copies, waits for them, and re-layouts: 21.5 us -> none  [the longest x2 10.8 us: padded(): lax.ppermute(lax.slice_in_dim(block, block.shape[dim] - width, None, axis...]
  transfers between devices with their start and end apart: 10 -> 9, of which waited for: 3 -> 5; matrix products, arithmetic and copies ran while one was open for 34% -> 3% of each run, Pallas kernels for 0% -> 10%
where the time goes in v1:
time: 226 us; the launch traced here: 225 us
  Pallas kernels  94.7 us (42%)
  blocking collectives  61.6 us (27%)
  starting transfers between devices  28.2 us (12%)
  waiting for transfers between devices  27.7 us (12%)
  local copies, waits for them, and re-layouts  6.96 us (3%)
  other arithmetic  5.35 us (2%)
    unnamed x1, blocking collectives  47 us
    pallas_call x1, Pallas kernels, observe(): pl.pallas_call(observe_kernel, in_specs=[smem] * 4 + [vmem] * 5, out_spec...  30.9 us
    pallas_call x1, Pallas kernels, gradient_of(): pl.pallas_call(gradient_kernel, grid=(f,), in_specs=[pl.BlockSpec((1, b,...  22.4 us
    ppermute x4, waiting for transfers between devices, exchange(): lax.ppermute(down, axis, backward)  21.7 us
    ppermute x4, starting transfers between devices, exchange(): lax.ppermute(up, axis, forward_pairs)  20.3 us
    pallas_call x1, Pallas kernels, forward(): pl.pallas_call(forward_kernel, grid=(f,), in_specs=[pl.BlockSpec((1, a, b...  16.2 us
    all_to_all x1, blocking collectives, body(): lax.all_to_all(labels.reshape(tiles, 3, most), axes, split_axis=0, concat...  14.6 us
    pallas_call x1, Pallas kernels, back_east(): pl.pallas_call(back_east_kernel, grid=(f,), in_specs=[full, rim, rim, pl....  9.49 us
  transfers between devices with their start and end apart: 9, of which 5 were waited for; matrix products, arithmetic and copies ran while one was open for 3% of the time, Pallas kernels for 10%

profile of v1, /device:TPU:0, one launch (start us, length us, event | category | flops | bytes accessed | tf_op | source)
XLA Modules:
  0.0 225.4 jit_solution(8081747868506599402)
XLA Ops:
  0.6 8.7 %pack_rows.1 = (f32[1024,4,128]{2,1,0:T(4,128)}, s32[3072]{0:T(1024)}) custom-call(s32[512]{0:T(512)} %owner.1, s32[512]{0:T(512)} %level.1, s32[512]{0:T(512)} %row.1, s32[512]{0:T(512)} %azimuth.1, f32[512,2,128]{2,1,0:T(2,128)} %inn.1, f32[512,2,128]{2,1,0:T(2,128)} %wt.1), custom_call_target="tpu_custom_call" | custom-call | tf_op jit(solution)/shard_map/pack_rows/pallas_call | solution.py:155
  9.4 0.8 reshape.24
  10.2 14.6 %all_to_all.10 = s32[32,3,32]{2,1,0:T(4,128)S(1)} all-to-all(s32[32,3,32]{2,1,0:T(4,128)S(1)} %reshape.24), channel_id=1, replica_groups=mesh['gx'=8,'gy'=4] {'gx','gy'}, dimensions={0} | all-to-all | bytes 24576 | tf_op jit(solution)/shard_map/all_to_all | solution.py:470
  24.8 2.7 %all-to-all-start.1 = ((f32[1024,4,128]{2,1,0:T(4,128)}), f32[1024,4,128]{2,1,0:T(4,128)S(1)}, u32[]{:S(2)}, u32[]{:S(2)}) async-start(f32[1024,4,128]{2,1,0:T(4,128)} %get-tuple-element.23), calls=%async_computation.1 | async-start | bytes 4194304 | tf_op jit(solution)/shard_map/all_to_all | solution.py:469
  27.5 6.9 %control_rims.1 = (f32[3,4,64,128]{3,2,1,0:T(8,128)}, f32[3,4,64,128]{3,2,1,0:T(8,128)}, f32[3,8,128]{2,1,0:T(8,128)}) custom-call(f32[3,64,64,128]{3,2,1,0:T(8,128)} %c_ref.3), custom_call_target="tpu_custom_call" | custom-call | tf_op jit(solution)/shard_map/control_rims/pallas_call | solution.py:191
  34.4 2.0 collective-permute-start
  36.5 1.3 collective-permute-start.1
  37.8 0.8 pad_maximum_fusion.vert
  38.6 2.9 %collective-permute-done.1.high = f32[3,4,64,128]{3,2,1,0:T(8,128)S(1)} collective-permute-done((f32[3,4,64,128]{3,2,1,0:T(8,128)}, f32[3,4,64,128]{3,2,1,0:T(8,128)S(1)}, u32[]{:S(2)}, u32[]{:S(2)}) %collective-permute-start.1) | collective-permute-done | bytes 393248 | tf_op jit(solution)/shard_map/ppermute | solution.py:446
  41.4 0.7 copy-done.6
  42.2 16.2 %forward.1 = (f32[3,64,64,128]{3,2,1,0:T(8,128)}, f32[3,8,64,128]{3,2,1,0:T(8,128)}, f32[3,8,64,128]{3,2,1,0:T(8,128)}) custom-call(f32[3,64,64,128]{3,2,1,0:T(8,128)} %c_ref.3, f32[3,4,64,128]{3,2,1,0:T(8,128)} %copy-done.5, f32[3,4,64,128]{3,2,1,0:T(8,128)} %copy-done.6, bf16[3,64,256]{2,1,0:T(8,128)(2,1)} %pad_maximum_fusion.vert, f32[3,9]{1,0:T(4,128)} %kernel_ref.6), custom_call_target="tpu_custom_call" | custom-call | tf_op jit(solution)/shard_map/forward/pallas_call | solution.py:234
  58.4 3.5 %collective-permute-start.2 = (f32[3,8,64,128]{3,2,1,0:T(8,128)}, f32[3,8,64,128]{3,2,1,0:T(8,128)S(1)}, u32[]{:S(2)}, u32[]{:S(2)}) collective-permute-start(f32[3,8,64,128]{3,2,1,0:T(8,128)} %get-tuple-element.21), channel_id=1, source_target_pairs={{0,1},{1,2},{2,3},{4,5},{5,6},{6,7},{8,9},{9,10},{10,11},{12,13},{... | collective-permute-start | bytes 2359304 | tf_op jit(solution)/shard_map/ppermute | solution.py:446
  61.9 1.3 collective-permute-start.3
  63.7 0.7 cos.6.cosine
  64.4 0.7 sin.6.sine
  65.1 0.7 add.8.cell
  65.8 5.8 %collective-permute-done.2.low = f32[3,8,64,128]{3,2,1,0:T(8,128)S(1)} collective-permute-done((f32[3,8,64,128]{3,2,1,0:T(8,128)}, f32[3,8,64,128]{3,2,1,0:T(8,128)S(1)}, u32[]{:S(2)}, u32[]{:S(2)}) %collective-permute-start.2) | collective-permute-done | bytes 786464 | tf_op jit(solution)/shard_map/ppermute | solution.py:446
  71.6 8.7 %collective-permute-done.3.high = f32[3,8,64,128]{3,2,1,0:T(8,128)} collective-permute-done((f32[3,8,64,128]{3,2,1,0:T(8,128)}, f32[3,8,64,128]{3,2,1,0:T(8,128)}, u32[]{:S(2)}, u32[]{:S(2)}) %collective-permute-start.3) | collective-permute-done | bytes 786464 | tf_op jit(solution)/shard_map/ppermute | solution.py:446
  80.3 1.3 copy-done
  81.6 30.9 %observe.1 = (f32[3,64,64,128]{3,2,1,0:T(8,128)}, f32[3,4,64,128]{3,2,1,0:T(8,128)}, f32[3,4,64,128]{3,2,1,0:T(8,128)}, f32[8,128]{1,0:T(8,128)}) custom-call(s32[1024]{0:T(1024)} %add.8.cell, f32[1024]{0:T(1024)} %cos.6.cosine, f32[1024]{0:T(1024)} %sin.6.sine, f32[3,9]{1,0:T(4,128)} %kernel_ref.7, f32[3,64,64,128]{3,2,1,0:T(8,128)} %get-tuple-element.20.u_ref, ...), custom_call_target="tpu_custom_call" | custom-call | tf_op jit(solution)/shard_map/observe/pallas_call | solution.py:339
  112.6 11.2 %collective-permute-start.4 = (f32[3,4,64,128]{3,2,1,0:T(8,128)}, f32[3,4,64,128]{3,2,1,0:T(8,128)S(1)}, u32[]{:S(2)}, u32[]{:S(2)}) collective-permute-start(f32[3,4,64,128]{3,2,1,0:T(8,128)} %get-tuple-element.25), channel_id=1, source_target_pairs={{0,4},{4,8},{8,12},{12,16},{16,20},{20,24},{24,28},{1,5},{5,9},{9,... | collective-permute-start | bytes 1179656 | tf_op jit(solution)/shard_map/ppermute | solution.py:446
  123.8 1.3 collective-permute-start.5
  125.3 10.2 %collective-permute-done.5.high = f32[3,4,64,128]{3,2,1,0:T(8,128)S(1)} collective-permute-done((f32[3,4,64,128]{3,2,1,0:T(8,128)}, f32[3,4,64,128]{3,2,1,0:T(8,128)S(1)}, u32[]{:S(2)}, u32[]{:S(2)}) %collective-permute-start.5) | collective-permute-done | bytes 393248 | tf_op jit(solution)/shard_map/ppermute | solution.py:446
  135.5 0.8 copy-done.8
  136.2 9.5 %back_east.1 = (f32[3,64,64,128]{3,2,1,0:T(8,128)}, f32[3,8,64,128]{3,2,1,0:T(8,128)}, f32[3,8,64,128]{3,2,1,0:T(8,128)}) custom-call(f32[3,64,64,128]{3,2,1,0:T(8,128)} %get-tuple-element.24.x_ref, f32[3,4,64,128]{3,2,1,0:T(8,128)} %copy-done.7, f32[3,4,64,128]{3,2,1,0:T(8,128)} %copy-done.8, f32[3,9]{1,0:T(4,128)} %kernel_ref.6), custom_call_target="tpu_custom_call" | custom-call | tf_op jit(solution)/shard_map/back_east/pallas_call | solution.py:375
  145.7 3.6 %collective-permute-start.6 = (f32[3,8,64,128]{3,2,1,0:T(8,128)}, f32[3,8,64,128]{3,2,1,0:T(8,128)S(1)}, u32[]{:S(2)}, u32[]{:S(2)}) collective-permute-start(f32[3,8,64,128]{3,2,1,0:T(8,128)} %get-tuple-element.28), channel_id=1, source_target_pairs={{0,1},{1,2},{2,3},{4,5},{5,6},{6,7},{8,9},{9,10},{10,11},{12,13},{... | collective-permute-start | bytes 2359304 | tf_op jit(solution)/shard_map/ppermute | solution.py:446
  149.3 1.3 collective-permute-start.7
  151.4 0.8 pad_maximum_fusion.1.vert
  152.7 1.4 maximum_dynamic-update-slice_fusion
  154.1 47.0 %all-reduce = f32[64]{0:T(128)S(1)} all-reduce(f32[64]{0:T(128)S(1)} %maximum_dynamic-update-slice_fusion), channel_id=2, replica_groups=mesh['gx'=8,'gy'=4] {'gx','gy'}, use_global_device_ids=true, to_apply=%add | all-reduce | flops 64 | bytes 512
  201.8 0.9 copy-done.2
  203.0 22.4 %gradient.1 = f32[3,4096,128]{2,1,0:T(8,128)} custom-call(f32[3,64,64,128]{3,2,1,0:T(8,128)} %get-tuple-element.27.x_ref, f32[3,8,64,128]{3,2,1,0:T(8,128)} %copy-done.2, f32[3,8,64,128]{3,2,1,0:T(8,128)} %copy-done.3, bf16[3,64,256]{2,1,0:T(8,128)(2,1)} %pad_maximum_fusion.1.vert, f32[3,9]{1,0:T(4,128)} %kernel_ref.7, f32[3,4096,128]{2,1,0:T(8,128)} %bitcast.7), custom_call_target="tpu_custom_call" | custom-call | tf_op jit(solution)/shard_map/gradient/pallas_call | solution.py:423
  (36 shorter events, 3.1 us)
Async XLA Ops:
  0.6 37.1 %copy-start.4 = (f32[3,64,64]{2,1,0:T(8,128)S(1)}, f32[3,64,64]{2,1,0:T(8,128)}, u32[]{:S(2)}) copy-start(f32[3,64,64]{2,1,0:T(8,128)} %param.16) | copy-start | bytes 147460
  24.8 55.5 %all-to-all-start.1 = ((f32[1024,4,128]{2,1,0:T(4,128)}), f32[1024,4,128]{2,1,0:T(4,128)S(1)}, u32[]{:S(2)}, u32[]{:S(2)}) async-start(f32[1024,4,128]{2,1,0:T(4,128)} %get-tuple-element.23), calls=%async_computation.1 | async-start | bytes 4194304 | tf_op jit(solution)/shard_map/all_to_all | solution.py:469
  34.4 4.1 %collective-permute-start = (f32[3,4,64,128]{3,2,1,0:T(8,128)}, f32[3,4,64,128]{3,2,1,0:T(8,128)S(1)}, u32[]{:S(2)}, u32[]{:S(2)}) collective-permute-start(f32[3,4,64,128]{3,2,1,0:T(8,128)} %get-tuple-element.18), channel_id=1, source_target_pairs={{0,4},{4,8},{8,12},{12,16},{16,20},{20,24},{24,28},{1,5},{5,9},{9,... | collective-permute-start | bytes 1179656 | tf_op jit(solution)/shard_map/ppermute | solution.py:446
  36.5 4.9 %collective-permute-start.1 = (f32[3,4,64,128]{3,2,1,0:T(8,128)}, f32[3,4,64,128]{3,2,1,0:T(8,128)S(1)}, u32[]{:S(2)}, u32[]{:S(2)}) collective-permute-start(f32[3,4,64,128]{3,2,1,0:T(8,128)} %get-tuple-element.19), channel_id=1, source_target_pairs={{4,0},{8,4},{12,8},{16,12},{20,16},{24,20},{28,24},{5,1},{9,5},{13... | collective-permute-start | bytes 1179656 | tf_op jit(solution)/shard_map/ppermute | solution.py:446
  38.6 2.9 %copy-start.5 = (f32[3,4,64,128]{3,2,1,0:T(8,128)}, f32[3,4,64,128]{3,2,1,0:T(8,128)S(1)}, u32[]{:S(2)}) copy-start(f32[3,4,64,128]{3,2,1,0:T(8,128)S(1)} %collective-permute-done.low) | copy-start | bytes 1179652
  41.4 0.7 copy-start.6
  58.4 13.2 %collective-permute-start.2 = (f32[3,8,64,128]{3,2,1,0:T(8,128)}, f32[3,8,64,128]{3,2,1,0:T(8,128)S(1)}, u32[]{:S(2)}, u32[]{:S(2)}) collective-permute-start(f32[3,8,64,128]{3,2,1,0:T(8,128)} %get-tuple-element.21), channel_id=1, source_target_pairs={{0,1},{1,2},{2,3},{4,5},{5,6},{6,7},{8,9},{9,10},{10,11},{12,13},{... | collective-permute-start | bytes 2359304 | tf_op jit(solution)/shard_map/ppermute | solution.py:446
  61.9 18.4 %collective-permute-start.3 = (f32[3,8,64,128]{3,2,1,0:T(8,128)}, f32[3,8,64,128]{3,2,1,0:T(8,128)}, u32[]{:S(2)}, u32[]{:S(2)}) collective-permute-start(f32[3,8,64,128]{3,2,1,0:T(8,128)} %get-tuple-element.22), channel_id=1, source_target_pairs={{1,0},{2,1},{3,2},{5,4},{6,5},{7,6},{9,8},{10,9},{11,10},{13,12},{... | collective-permute-start | bytes 2359304 | tf_op jit(solution)/shard_map/ppermute | solution.py:446
  71.6 8.7 %copy-start.1 = (f32[3,8,64,128]{3,2,1,0:T(8,128)}, f32[3,8,64,128]{3,2,1,0:T(8,128)S(1)}, u32[]{:S(2)}) copy-start(f32[3,8,64,128]{3,2,1,0:T(8,128)S(1)} %collective-permute-done.2.low) | copy-start | bytes 2359300
  80.3 1.4 copy-start
  81.6 69.1 %copy-start.9 = (f32[3,8,128]{2,1,0:T(8,128)S(1)}, f32[3,8,128]{2,1,0:T(8,128)}, u32[]{:S(2)}) copy-start(f32[3,8,128]{2,1,0:T(8,128)} %get-tuple-element.30) | copy-start | bytes 36868
  112.6 39.6 %copy-start.10 = (f32[8,128]{1,0:T(8,128)S(1)}, f32[8,128]{1,0:T(8,128)}, u32[]{:S(2)}) copy-start(f32[8,128]{1,0:T(8,128)} %get-tuple-element.31) | copy-start | bytes 12292
  112.6 88.7 %copy-start.11 = (f32[2]{0:T(128)S(1)}, f32[2]{0:T(128)}, u32[]{:S(2)}) copy-start(f32[2]{0:T(128)} %constant.11) | copy-start | bytes 28
  112.6 12.7 %collective-permute-start.4 = (f32[3,4,64,128]{3,2,1,0:T(8,128)}, f32[3,4,64,128]{3,2,1,0:T(8,128)S(1)}, u32[]{:S(2)}, u32[]{:S(2)}) collective-permute-start(f32[3,4,64,128]{3,2,1,0:T(8,128)} %get-tuple-element.25), channel_id=1, source_target_pairs={{0,4},{4,8},{8,12},{12,16},{16,20},{20,24},{24,28},{1,5},{5,9},{9,... | collective-permute-start | bytes 1179656 | tf_op jit(solution)/shard_map/ppermute | solution.py:446
  123.8 11.7 %collective-permute-start.5 = (f32[3,4,64,128]{3,2,1,0:T(8,128)}, f32[3,4,64,128]{3,2,1,0:T(8,128)S(1)}, u32[]{:S(2)}, u32[]{:S(2)}) collective-permute-start(f32[3,4,64,128]{3,2,1,0:T(8,128)} %get-tuple-element.26), channel_id=1, source_target_pairs={{4,0},{8,4},{12,8},{16,12},{20,16},{24,20},{28,24},{5,1},{9,5},{13... | collective-permute-start | bytes 1179656 | tf_op jit(solution)/shard_map/ppermute | solution.py:446
  125.3 10.2 %copy-start.7 = (f32[3,4,64,128]{3,2,1,0:T(8,128)}, f32[3,4,64,128]{3,2,1,0:T(8,128)S(1)}, u32[]{:S(2)}) copy-start(f32[3,4,64,128]{3,2,1,0:T(8,128)S(1)} %collective-permute-done.4.low) | copy-start | bytes 1179652
  135.5 0.8 copy-start.8
  145.7 56.1 %collective-permute-start.6 = (f32[3,8,64,128]{3,2,1,0:T(8,128)}, f32[3,8,64,128]{3,2,1,0:T(8,128)S(1)}, u32[]{:S(2)}, u32[]{:S(2)}) collective-permute-start(f32[3,8,64,128]{3,2,1,0:T(8,128)} %get-tuple-element.28), channel_id=1, source_target_pairs={{0,1},{1,2},{2,3},{4,5},{5,6},{6,7},{8,9},{9,10},{10,11},{12,13},{... | collective-permute-start | bytes 2359304 | tf_op jit(solution)/shard_map/ppermute | solution.py:446
  149.3 52.5 %collective-permute-start.7 = (f32[3,8,64,128]{3,2,1,0:T(8,128)}, f32[3,8,64,128]{3,2,1,0:T(8,128)S(1)}, u32[]{:S(2)}, u32[]{:S(2)}) collective-permute-start(f32[3,8,64,128]{3,2,1,0:T(8,128)} %get-tuple-element.29), channel_id=1, source_target_pairs={{1,0},{2,1},{3,2},{5,4},{6,5},{7,6},{9,8},{10,9},{11,10},{13,12},{... | collective-permute-start | bytes 2359304 | tf_op jit(solution)/shard_map/ppermute | solution.py:446
  201.8 0.9 copy-start.2
  201.8 1.1 copy-start.3

commit v2 on v1

v2 whole, which is shorter than its diff:
```python
import functools
import math

import jax
import jax.numpy as jnp
from jax import lax
from jax.experimental import pallas as pl
from jax.experimental.pallas import tpu as pltpu
from jax.sharding import PartitionSpec as P

F32 = jnp.float32
BF16 = jnp.bfloat16
VMEM_BYTES = 56 * 1024 * 1024


def params():
    return pltpu.CompilerParams(vmem_limit_bytes=VMEM_BYTES)


def split(value):
    high = value.astype(BF16)
    low = (value - high.astype(F32)).astype(BF16)
    return high, low


def doubled(weights):
    high, low = split(weights)
    row = jnp.concatenate([high, low], axis=1)
    return jnp.concatenate([row, row], axis=0)


def times(rows, weights):
    high, low = split(rows)
    both = jnp.dot(
        jnp.concatenate([high, low], axis=1), weights, preferred_element_type=F32
    )
    half = both.shape[1] // 2
    return both[:, :half] + both[:, half:]


def taps_at(kernel_ref, f, distance, allowed):
    total = jnp.zeros(distance.shape, F32)
    for d in range(kernel_ref.shape[1]):
        total = jnp.where(distance == d, kernel_ref[f, d], total)
    return jnp.where(allowed, total, 0.0)


def main_band(kernel_ref, f):
    r = lax.broadcasted_iota(jnp.int32, (128, 128), 0)
    c = lax.broadcasted_iota(jnp.int32, (128, 128), 1)
    return doubled(taps_at(kernel_ref, f, jnp.abs(r - c), jnp.abs(r - c) <= 8))


def rim_band(kernel_ref, f, offset):
    r = (lax.broadcasted_iota(jnp.int32, (128, 128), 0) + (128 - offset)) & 127
    c = (lax.broadcasted_iota(jnp.int32, (128, 128), 1) + (128 - offset)) & 127
    distance = jnp.abs(r - c)
    fits = ((r >> 4) == (c >> 4)) & ((r & 8) != (c & 8)) & (distance <= 8)
    return doubled(taps_at(kernel_ref, f, distance, fits))


def pack_rims(get, put_right, put_left, groups, b):
    lane = lax.broadcasted_iota(jnp.int32, (b, 128), 1)
    first = (lane & 8) == 0

    def one(g, carry):
        even = jnp.zeros((b, 128), F32)
        odd = jnp.zeros((b, 128), F32)
        for q in range(8):
            even = jnp.where(
                (lane >> 4) == q, pltpu.roll(get(16 * g + 2 * q), (16 * q + 8) % 128, 1), even
            )
            odd = jnp.where(
                (((lane + 120) & 127) >> 4) == q,
                pltpu.roll(get(16 * g + 2 * q + 1), (16 * q + 16) % 128, 1),
                odd,
            )
        put_right(g, jnp.where(first, even, odd))
        put_left(g, jnp.where(first, odd, even))
        return carry

    lax.fori_loop(0, groups, one, 0)


def east_filter(get, low_ref, high_ref, put, kernel_ref, f, groups, b):
    band = main_band(kernel_ref, f)
    rim_even = rim_band(kernel_ref, f, 0)
    rim_odd = rim_band(kernel_ref, f, 8)
    lane = lax.broadcasted_iota(jnp.int32, (b, 128), 1)
    first = (lane & 8) == 0
    edge = (lane < 8) | (lane >= 120)

    def one(g, carry):
        low = low_ref[f, g]
        high = high_ref[f, g]
        even = times(jnp.where(first, low, high), rim_even)
        odd = times(jnp.where(first, high, low), rim_odd)
        for part in range(2):
            many = jnp.concatenate([get(16 * g + 8 * part + j) for j in range(8)], axis=0)
            flat = times(many, band)
            for j in range(4):
                q = 4 * part + j
                at = 16 * g + 2 * q
                own = flat[2 * j * b : (2 * j + 1) * b]
                put(at, own + jnp.where(edge, pltpu.roll(even, (248 - 16 * q) % 128, 1), 0.0))
                own = flat[(2 * j + 1) * b : (2 * j + 2) * b]
                put(at + 1, own + jnp.where(edge, pltpu.roll(odd, (240 - 16 * q) % 128, 1), 0.0))
        return carry

    lax.fori_loop(0, groups, one, 0)


def north_filter(slab_ref, kernel_ref, f, y0, kb):
    u = slab_ref[f, pl.ds(y0, 24), pl.ds(kb, 8), :]
    total = kernel_ref[f, 0] * u[8:16]
    for d in range(1, 9):
        total = total + kernel_ref[f, d] * (u[8 - d : 16 - d] + u[8 + d : 16 + d])
    return total


def fold_rows(x):
    return jnp.sum(x.reshape(-1, 8, 128), axis=0)


def rows_kernel(most, owner, level, row, azimuth, inn, wt, out, labels, count):
    rows = owner.shape[0]
    tiles = count.shape[0]
    out[...] = jnp.zeros_like(out)

    def clear(t, carry):
        count[t] = 0
        for j in range(3 * most):
            labels[t * 3 * most + j] = 0
        return carry

    lax.fori_loop(0, tiles, clear, 0)

    def one(i, carry):
        for j in range(4):
            r = i * 4 + j
            o = owner[r]
            rank = count[o]
            count[o] = rank + 1
            slot = o * most + rank
            labels[slot * 3] = level[r]
            labels[slot * 3 + 1] = row[r]
            labels[slot * 3 + 2] = azimuth[r]
            out[slot, 0:2] = inn[r]
            out[slot, 2:4] = wt[r]
        return carry

    lax.fori_loop(0, rows // 4, one, 0)


def pack_rows(owner, level, row, azimuth, inn, wt, tiles, most):
    smem = pl.BlockSpec(memory_space=pltpu.SMEM)
    vmem = pl.BlockSpec(memory_space=pltpu.VMEM)
    return pl.pallas_call(
        functools.partial(rows_kernel, most),
        out_shape=(
            jax.ShapeDtypeStruct((tiles * most, 4, 128), F32),
            jax.ShapeDtypeStruct((tiles * 3 * most,), jnp.int32),
        ),
        in_specs=[smem] * 4 + [vmem] * 2,
        out_specs=(vmem, smem),
        scratch_shapes=[pltpu.SMEM((tiles,), jnp.int32)],
        compiler_params=params(),
        name="pack_rows",
    )(owner, level, row, azimuth, inn, wt)


def send(src, dst, sems, which, f, axis, target):
    return pltpu.make_async_remote_copy(
        src_ref=src.at[f],
        dst_ref=dst.at[f],
        send_sem=sems.at[0, which, f],
        recv_sem=sems.at[1, which, f],
        device_id={axis: target},
        device_id_type=pl.DeviceIdType.MESH,
    )


def sweep_kernel(
    nx, ny, first, x_ref, east, north, extra, extra2, out, total_out,
    xbuf, right, left, low, high, slab, flat, fill_sems, sems, parts, sum_sems,
):
    fields, a, b, w = x_ref.shape
    ys, ks = slab.shape[1] - 16, slab.shape[2]
    ix = lax.axis_index("gx")
    iy = lax.axis_index("gy")
    up_x, down_x = jnp.minimum(ix + 1, nx - 1), jnp.maximum(ix - 1, 0)
    up_y, down_y = jnp.minimum(iy + 1, ny - 1), jnp.maximum(iy - 1, 0)
    has_up_x, has_down_x = ix < nx - 1, ix > 0
    has_up_y, has_down_y = iy < ny - 1, iy > 0

    def fill(f):
        return pltpu.make_async_copy(x_ref.at[f], xbuf.at[f], fill_sems.at[f])

    for f in range(fields):
        fill(f).start()

    barrier = pltpu.get_barrier_semaphore()

    def greet(axis, peer):
        pl.semaphore_signal(
            barrier, inc=1, device_id={axis: peer}, device_id_type=pl.DeviceIdType.MESH
        )

    if first:
        for axis, peer, there in (
            ("gx", up_x, has_up_x),
            ("gx", down_x, has_down_x),
            ("gy", up_y, has_up_y),
            ("gy", down_y, has_down_y),
        ):

            @pl.when(there)
            def _():
                greet(axis, peer)

        beside = jnp.minimum(ix, 1) + jnp.minimum(nx - 1 - ix, 1)
        around = jnp.minimum(iy, 1) + jnp.minimum(ny - 1 - iy, 1)
        pl.semaphore_wait(barrier, beside + around)
    else:
        for j in range(1, nx):
            greet("gx", lax.rem(ix + j, nx))
        for j in range(1, ny):
            greet("gy", lax.rem(iy + j, ny))
        pl.semaphore_wait(barrier, nx + ny - 2)

    @pl.when(jnp.logical_not(has_down_x))
    def _():
        low[...] = jnp.zeros_like(low)

    @pl.when(jnp.logical_not(has_up_x))
    def _():
        high[...] = jnp.zeros_like(high)

    @pl.when(jnp.logical_not(has_down_y))
    def _():
        slab[:, 0:8] = jnp.zeros((fields, 8, ks, w), F32)

    @pl.when(jnp.logical_not(has_up_y))
    def _():
        slab[:, ys + 8 :] = jnp.zeros((fields, 8, ks, w), F32)

    def to_up_x(f):
        return send(right, low, sems, 0, f, "gx", up_x)

    def to_down_x(f):
        return send(left, high, sems, 1, f, "gx", down_x)

    def edge_copy(f, which, src, dst, target):
        return pltpu.make_async_remote_copy(
            src_ref=slab.at[f, pl.ds(src, 8)],
            dst_ref=slab.at[f, pl.ds(dst, 8)],
            send_sem=sems.at[0, which, f],
            recv_sem=sems.at[1, which, f],
            device_id={"gy": target},
            device_id_type=pl.DeviceIdType.MESH,
        )

    def to_up_y(f):
        return edge_copy(f, 2, ys, 0, up_y)

    def to_down_y(f):
        return edge_copy(f, 3, 8, ys + 8, down_y)

    def share(axis, n, slot, peer, row):
        return pltpu.make_async_remote_copy(
            src_ref=parts.at[row, slot],
            dst_ref=parts.at[row, slot],
            send_sem=sum_sems.at[0, row, peer],
            recv_sem=sum_sems.at[1, row, slot],
            device_id={axis: peer},
            device_id_type=pl.DeviceIdType.MESH,
        )

    def arrival(axis, peer, row):
        return pltpu.make_async_remote_copy(
            src_ref=parts.at[row, peer],
            dst_ref=parts.at[row, peer],
            send_sem=sum_sems.at[0, row, peer],
            recv_sem=sum_sems.at[1, row, peer],
            device_id={axis: peer},
            device_id_type=pl.DeviceIdType.MESH,
        )

    if not first:
        parts[0, ix] = extra[...]
        for j in range(1, nx):
            share("gx", nx, ix, lax.rem(ix + j, nx), 0).start()

    def pack(f, carry):
        fill(f).wait()

        def put_right(g, v):
            right[f, g] = v

        def put_left(g, v):
            left[f, g] = v

        pack_rims(lambda s: xbuf[f, s], put_right, put_left, a // 16, b)

        @pl.when(has_up_x)
        def _():
            to_up_x(f).start()

        @pl.when(has_down_x)
        def _():
            to_down_x(f).start()

        return carry

    lax.fori_loop(0, fields, pack, 0)

    if first:

        def square(i, total):
            v = xbuf[i // a, i % a]
            return total + fold_rows(v * v)

        total_out[...] = lax.fori_loop(0, fields * a, square, jnp.zeros((8, w), F32))
    else:
        for j in range(1, nx):
            arrival("gx", lax.rem(ix + j, nx), 0).wait_recv()
        row_sum = parts[0, 0]
        for j in range(1, nx):
            row_sum = row_sum + parts[0, j]
        parts[1, iy] = row_sum
        for j in range(1, ny):
            share("gy", ny, iy, lax.rem(iy + j, ny), 1).start()

    def middle(f, carry):
        @pl.when(has_down_x)
        def _():
            to_up_x(f).wait_recv()

        @pl.when(has_up_x)
        def _():
            to_down_x(f).wait_recv()

        if first:
            pitch = b + 8

            def put(s, v):
                flat[pl.ds(pl.multiple_of(s * pitch, 8), b), :] = v

            east_filter(lambda s: xbuf[f, s], low, high, put, east, f, a // 16, b)
            v = extra[f]

            def one(p, carry):
                for j in range(4):
                    y = p * 8 + 2 * j
                    x = jnp.concatenate(
                        [flat[pl.ds(y, a, stride=pitch), :], flat[pl.ds(y + 1, a, stride=pitch), :]],
                        axis=1,
                    )
                    h, l = split(x)
                    r = jnp.dot(
                        v, jnp.concatenate([h, l, h, l], axis=0), preferred_element_type=F32
                    )
                    slab[f, 8 + y] = r[:, :w]
                    slab[f, 9 + y] = r[:, w:]
                return carry

            lax.fori_loop(0, b // 8, one, 0)
        else:

            def put_slab(s, v):
                slab[f, 8 + s] = v

            east_filter(lambda s: xbuf[f, s], low, high, put_slab, east, f, a // 16, b)

        @pl.when(has_up_y)
        def _():
            to_up_y(f).start()

        @pl.when(has_down_y)
        def _():
            to_down_y(f).start()

        return carry

    lax.fori_loop(0, fields, middle, 0)

    def last(f, carry):
        @pl.when(has_down_y)
        def _():
            to_up_y(f).wait_recv()

        @pl.when(has_up_y)
        def _():
            to_down_y(f).wait_recv()

        def one(i, carry):
            y0 = (i // (ks // 8)) * 8
            kb = pl.multiple_of((i % (ks // 8)) * 8, 8)
            total = north_filter(slab, north, f, y0, kb)
            for j in range(8):
                value = total[j]
                if first:
                    value = value * extra2[f, pl.ds(y0 + j, 1), :]
                out[f, y0 + j, pl.ds(kb, 8), :] = value
            return carry

        lax.fori_loop(0, (ys // 8) * (ks // 8), one, 0)
        return carry

    lax.fori_loop(0, fields, last, 0)

    if not first:
        for j in range(1, ny):
            arrival("gy", lax.rem(iy + j, ny), 1).wait_recv()
        all_sum = parts[1, 0]
        for j in range(1, ny):
            all_sum = all_sum + parts[1, j]
        total_out[...] = all_sum
        for j in range(1, nx):
            share("gx", nx, ix, lax.rem(ix + j, nx), 0).wait_send()
        for j in range(1, ny):
            share("gy", ny, iy, lax.rem(iy + j, ny), 1).wait_send()

    def drain(f, carry):
        @pl.when(has_up_x)
        def _():
            to_up_x(f).wait_send()

        @pl.when(has_down_x)
        def _():
            to_down_x(f).wait_send()

        @pl.when(has_up_y)
        def _():
            to_up_y(f).wait_send()

        @pl.when(has_down_y)
        def _():
            to_down_y(f).wait_send()

        return carry

    lax.fori_loop(0, fields, drain, 0)


def sweep(first, x, east, north, extra, extra2):
    f, a, b, w = x.shape
    nx, ny = lax.axis_size("gx"), lax.axis_size("gy")
    ys, ks = (b, a) if first else (a, b)
    smem = pl.BlockSpec(memory_space=pltpu.SMEM)
    vmem = pl.BlockSpec(memory_space=pltpu.VMEM)
    rim = pltpu.VMEM((f, a // 16, b, w), F32)
    total = (8, w) if first else (2, 8, w)
    return pl.pallas_call(
        functools.partial(sweep_kernel, nx, ny, first),
        in_specs=[pl.BlockSpec(memory_space=pl.ANY), smem, smem, vmem, vmem],
        out_specs=(vmem, vmem),
        out_shape=(
            jax.ShapeDtypeStruct((f, ys, ks, w), F32),
            jax.ShapeDtypeStruct(total, F32),
        ),
        scratch_shapes=[
            pltpu.VMEM((f, a, b, w), F32),
            rim,
            rim,
            rim,
            rim,
            pltpu.VMEM((f, ys + 16, ks, w), F32),
            pltpu.VMEM((a * (b + 8), w), F32),
            pltpu.SemaphoreType.DMA((f,)),
            pltpu.SemaphoreType.DMA((2, 4, f)),
            pltpu.VMEM((2, max(nx, ny), 2, 8, w), F32),
            pltpu.SemaphoreType.DMA((2, 2, max(nx, ny))),
        ],
        compiler_params=pltpu.CompilerParams(
            vmem_limit_bytes=VMEM_BYTES,
            collective_id=0 if first else 1,
            has_side_effects=True,
        ),
        name="sweep_forward" if first else "sweep_back",
    )(x, east, north, extra, extra2)


def observe_kernel(
    cell, cosine, sine, s_ref, spread, rows_ref, adj, obs, a0, a1, a2, m0, m1
):
    fields, b, w = spread.shape
    a = s_ref.shape[1] // b
    s0, s1, s2 = s_ref.at[0], s_ref.at[1], s_ref.at[2]
    adjs = (a0, a1, a2)
    for f in range(fields):
        adjs[f][...] = jnp.zeros_like(a0)

    count = rows_ref.shape[0]

    def pick(i, carry):
        for j in range(8):
            r = i * 8 + j
            at = cell[r]
            m0[pl.ds(r, 1), :] = cosine[r] * s0[pl.ds(at, 1), :] + sine[r] * s1[pl.ds(at, 1), :]
            m1[pl.ds(r, 1), :] = s2[pl.ds(at, 1), :]
        return carry

    lax.fori_loop(0, count // 8, pick, 0)

    def weigh(i, total):
        at = pl.ds(pl.multiple_of(i * 8, 8), 8)
        d0 = m0[at, :] - rows_ref[at, 0, :]
        d1 = m1[at, :] - rows_ref[at, 1, :]
        w0 = rows_ref[at, 2, :] * d0
        w1 = rows_ref[at, 3, :] * d1
        m0[at, :] = w0
        m1[at, :] = w1
        return total + (w0 * d0 + w1 * d1)

    obs[...] = lax.fori_loop(0, count // 8, weigh, jnp.zeros((8, w), F32))

    def push(i, carry):
        for j in range(8):
            r = i * 8 + j
            at = pl.ds(cell[r], 1)
            w0 = m0[pl.ds(r, 1), :]
            a0[at, :] = a0[at, :] + cosine[r] * w0
            a1[at, :] = a1[at, :] + sine[r] * w0
            a2[at, :] = a2[at, :] + m1[pl.ds(r, 1), :]
        return carry

    lax.fori_loop(0, count // 8, push, 0)
    for f in range(fields):
        grown = adjs[f]

        def scale_rows(y, carry):
            at = pl.ds(pl.multiple_of(y * a, a), a)
            adj[f, y] = grown[at, :] * spread[f, pl.ds(y, 1), :]
            return carry

        lax.fori_loop(0, b, scale_rows, 0)


def observe(cell, cosine, sine, state, spread, rows):
    f, b, w = spread.shape
    cells = state.shape[1]
    smem = pl.BlockSpec(memory_space=pltpu.SMEM)
    vmem = pl.BlockSpec(memory_space=pltpu.VMEM)
    return pl.pallas_call(
        observe_kernel,
        in_specs=[smem] * 3 + [vmem] * 3,
        out_specs=(vmem, vmem),
        out_shape=(
            jax.ShapeDtypeStruct((f, b, cells // b, w), F32),
            jax.ShapeDtypeStruct((8, w), F32),
        ),
        scratch_shapes=[pltpu.VMEM((cells, w), F32)] * 3
        + [pltpu.VMEM((rows.shape[0], w), F32)] * 2,
        compiler_params=params(),
        name="observe",
    )(cell, cosine, sine, state, spread, rows)


def gradient_kernel(x_ref, vert, c_ref, out, flat):
    b, a, w = x_ref.shape[1:]
    pitch = b + 8
    v = vert[0]
    for j in range(b // 2):
        x = jnp.concatenate([x_ref[0, 2 * j], x_ref[0, 2 * j + 1]], axis=1)
        h, l = split(x)
        r = jnp.dot(v, jnp.concatenate([h, l, h, l], axis=0), preferred_element_type=F32)
        flat[pl.ds(2 * j, a, stride=pitch), :] = r[:, :w]
        flat[pl.ds(2 * j + 1, a, stride=pitch), :] = r[:, w:]
    for s in range(a):
        out[0, s] = c_ref[0, s] + flat[s * pitch : s * pitch + b, :]


def gradient_of(x, vert, control):
    f, b, a, w = x.shape
    rows = 16
    tall = pl.BlockSpec((1, a, rows, w), lambda i, j: (i, 0, j, 0))
    return pl.pallas_call(
        gradient_kernel,
        grid=(f, b // rows),
        in_specs=[
            pl.BlockSpec((1, rows, a, w), lambda i, j: (i, j, 0, 0)),
            pl.BlockSpec((1, a, 4 * a), lambda i, j: (i, 0, 0)),
            tall,
        ],
        out_specs=tall,
        out_shape=jax.ShapeDtypeStruct(control.shape, F32),
        scratch_shapes=[pltpu.VMEM((a * (rows + 8), w), F32)],
        compiler_params=params(),
        name="gradient",
    )(x, vert, control)


def vertical_parts(v):
    high = lax.reduce_precision(v, 8, 7)
    low = lax.reduce_precision(v - high, 8, 7)
    return jnp.concatenate([high, high, low, low], axis=2).astype(BF16)


def body(
    control, spread, kernel_east, kernel_north, vertical,
    tile_owner, gate_level, tile_row, beam_azimuth, innovation, obs_weight,
):
    tiles = lax.axis_size("gx") * lax.axis_size("gy")
    most = 2 * tile_owner.shape[0] // tiles
    levels = control.shape[1]
    axes = ("gx", "gy")

    rows, labels = pack_rows(
        tile_owner, gate_level, tile_row, beam_azimuth, innovation, obs_weight, tiles, most
    )
    rows = lax.all_to_all(rows, axes, split_axis=0, concat_axis=0, tiled=True)
    labels = lax.all_to_all(
        labels.reshape(tiles * most, 3), axes, split_axis=0, concat_axis=0, tiled=True
    )
    vert = vertical_parts(vertical)
    vert_back = vertical_parts(jnp.swapaxes(vertical, 1, 2))
    state, square = sweep(True, control, kernel_east, kernel_north, vert, spread)
    cell = labels[:, 1] * levels + labels[:, 0]
    angle = labels[:, 2].astype(F32) * (2.0 * math.pi / 360.0)
    adj, obs = observe(
        cell,
        jnp.cos(angle),
        jnp.sin(angle),
        state.reshape(state.shape[0], -1, state.shape[3]),
        spread,
        rows,
    )
    parts = jnp.stack([square, obs])
    smooth, totals = sweep(False, adj, kernel_east, kernel_north, parts, spread)
    counts = jnp.array([control.size * tiles, innovation.size * tiles], F32)
    cost = 0.5 * jnp.sum(totals, axis=(1, 2)) / counts
    return gradient_of(smooth, vert_back, control), cost


def solution(mesh):
    both = ("gx", "gy")
    placed = (
        P(None, None, "gy", "gx"),
        P(None, "gy", "gx"),
        P(),
        P(),
        P(),
        P(both),
        P(both),
        P(both),
        P(both),
        P(both, None, None),
        P(both, None, None),
    )
    return jax.shard_map(
        body,
        mesh=mesh,
        in_specs=placed,
        out_specs=(P(None, None, "gy", "gx"), P()),
        check_vma=False,
    )
```

time: 226 us -> 169 us (0.75)
  blocking collectives: 61.6 us -> 14.6 us
  Pallas kernels: 94.7 us -> 141 us
  waiting for transfers between devices: 27.7 us -> 0.01 us
  starting transfers between devices: 28.2 us -> 2.73 us
  local copies, waits for them, and re-layouts: 6.96 us -> 2.87 us
    unnamed x1 -> x0, blocking collectives: 47 us -> none
    pallas_call x5 -> x4, Pallas kernels: 86 us -> 133 us  [the longest x2 103 us: sweep(): pl.pallas_call(functools.partial(sweep_kernel, nx, ny, first), in_specs=[...]
    ppermute x8 -> x0, waiting for transfers between devices: 27.7 us -> none  [the longest x4 21.7 us: exchange(): lax.ppermute(down, axis, backward)]
    ppermute x8 -> x0, starting transfers between devices: 25.5 us -> none  [the longest x4 20.3 us: exchange(): lax.ppermute(up, axis, forward_pairs)]
    unnamed x26 -> x11, local copies, waits for them, and re-layouts: 4.1 us -> 1.46 us
  transfers between devices with their start and end apart: 9 -> 1, of which waited for: 5 -> 0; matrix products, arithmetic and copies ran while one was open for 3% -> 2% of each run, Pallas kernels for 10% -> 35%
where the time goes in v2:
time: 169 us; the launch traced here: 166 us
  Pallas kernels  141 us (83%)
  blocking collectives  14.6 us (9%)
  other arithmetic  4.76 us (3%)
  local copies, waits for them, and re-layouts  2.87 us (2%)
  starting transfers between devices  2.73 us (2%)
    pallas_call x2, Pallas kernels, sweep(): pl.pallas_call(functools.partial(sweep_kernel, nx, ny, first), in_specs=[...  103 us
    pallas_call x1, Pallas kernels, observe(): pl.pallas_call(observe_kernel, in_specs=[smem] * 3 + [vmem] * 3, out_spec...  17.5 us
    all_to_all x1, blocking collectives, body(): lax.all_to_all(labels.reshape(tiles * most, 3), axes, split_axis=0, conca...  14.6 us
    pallas_call x1, Pallas kernels, gradient_of(): pl.pallas_call(gradient_kernel, grid=(f, b // rows), in_specs=[pl.BlockSp...  12.3 us
    pallas_call x1, Pallas kernels, pack_rows(): pl.pallas_call(functools.partial(rows_kernel, most), out_shape=(jax.Shape...  7.96 us
  transfers between devices with their start and end apart: 1, of which 0 were waited for; matrix products, arithmetic and copies ran while one was open for 2% of the time, Pallas kernels for 35%

profile of v2, /device:TPU:0, one launch (start us, length us, event | category | flops | bytes accessed | tf_op | source)
XLA Modules:
  0.0 166.2 jit_solution(1541756671481298259)
XLA Ops:
  0.6 0.0 copy-start.1
  0.6 8.0 %pack_rows.1 = (f32[1024,4,128]{2,1,0:T(4,128)}, s32[3072]{0:T(1024)}) custom-call(s32[512]{0:T(512)} %owner.1, s32[512]{0:T(512)} %level.1, s32[512]{0:T(512)} %row.1, s32[512]{0:T(512)} %azimuth.1, f32[512,2,128]{2,1,0:T(2,128)} %inn.1, f32[512,2,128]{2,1,0:T(2,128)} %wt.1), custom_call_target="tpu_custom_call" | custom-call | tf_op jit(solution)/shard_map/pack_rows/pallas_call | solution.py:158
  8.6 1.1 all_to_all.11
  9.7 0.3 copy.21
  9.9 14.6 %all_to_all.17 = s32[32,32,3]{1,2,0:T(4,128)S(1)} all-to-all(s32[32,32,3]{1,2,0:T(4,128)S(1)} %copy.21), channel_id=1, replica_groups=mesh['gx'=8,'gy'=4] {'gx','gy'}, dimensions={0} | all-to-all | bytes 24576 | tf_op jit(solution)/shard_map/all_to_all | solution.py:613
  24.5 2.7 %all-to-all-start.1 = ((f32[1024,4,128]{2,1,0:T(4,128)}), f32[1024,4,128]{2,1,0:T(4,128)S(1)}, u32[]{:S(2)}, u32[]{:S(2)}) async-start(f32[1024,4,128]{2,1,0:T(4,128)} %get-tuple-element.12), calls=%async_computation.1 | async-start | bytes 4194304 | tf_op jit(solution)/shard_map/all_to_all | solution.py:612
  27.3 0.0 copy-done.1
  27.3 0.1 copy.23
  27.4 0.7 pad_maximum_fusion.extra
  28.2 58.8 %sweep_forward.1 = (f32[3,64,64,128]{3,2,1,0:T(8,128)}, f32[8,128]{1,0:T(8,128)}) custom-call(f32[3,64,64,128]{3,2,1,0:T(8,128)} %c_ref.1, f32[3,9]{1,0:T(4,128)} %east.3, f32[3,9]{1,0:T(4,128)} %north.3, bf16[3,64,256]{2,1,0:T(8,128)(2,1)} %pad_maximum_fusion.extra, f32[3,64,128]{2,1,0:T(8,128)} %extra2.3), custom_call_target="tpu_custom_call" | custom-call | tf_op jit(solution)/shard_map/sweep_forward/pallas_call | solution.py:454
  87.0 0.0 copy-start.3
  87.0 0.8 pad_maximum_fusion.1.vert
  87.8 0.1 all_to_all.13
  87.8 0.6 slice_add_fusion
  88.5 0.7 fusion.5
  89.2 0.0 all-to-all-done.1.rows_ref
  89.2 0.0 copy-start
  89.2 1.3 copy-done
  90.5 17.5 %observe.1 = (f32[3,64,64,128]{3,2,1,0:T(8,128)}, f32[8,128]{1,0:T(8,128)}) custom-call(s32[1024]{0:T(1024)} %bitcast.12, f32[1024]{0:T(1024)} %bitcast.14, f32[1024]{0:T(1024)} %bitcast.13, f32[3,4096,128]{2,1,0:T(8,128)} %bitcast.11, f32[3,64,128]{2,1,0:T(8,128)} %extra2.3, f32[1024,4,128]{2,1,0:T(4,128)} %copy-done), custom_call_target="tpu_custom_call" | custom-call | tf_op jit(solution)/shard_map/observe/pallas_call | solution.py:545
  108.1 0.0 copy-done.3
  108.1 1.3 pad_maximum_fusion.2.extra
  109.4 43.9 %sweep_back.1 = (f32[3,64,64,128]{3,2,1,0:T(8,128)}, f32[2,8,128]{2,1,0:T(8,128)}) custom-call(f32[3,64,64,128]{3,2,1,0:T(8,128)} %get-tuple-element.13.x_ref, f32[3,9]{1,0:T(4,128)} %east.3, f32[3,9]{1,0:T(4,128)} %north.3, f32[2,8,128]{2,1,0:T(8,128)} %pad_maximum_fusion.2.extra, f32[3,64,128]{2,1,0:T(8,128)} %extra2.3), custom_call_target="tpu_custom_call" | custom-call | tf_op jit(solution)/shard_map/sweep_back/pallas_call | solution.py:454
  153.3 0.0 copy-start.2
  153.3 0.0 copy-start.4
  153.3 12.3 %gradient.1 = f32[3,64,64,128]{3,2,1,0:T(8,128)} custom-call(f32[3,64,64,128]{3,2,1,0:T(8,128)} %get-tuple-element.16.x_ref, bf16[3,64,256]{2,1,0:T(8,128)(2,1)} %pad_maximum_fusion.1.vert, f32[3,64,64,128]{3,2,1,0:T(8,128)} %c_ref.1), custom_call_target="tpu_custom_call" | custom-call | tf_op jit(solution)/shard_map/gradient/pallas_call | solution.py:578
  165.6 0.0 copy-done.2
  165.6 0.1 reduce_sum.9
  165.7 0.0 copy-done.4
  165.7 0.5 multiply_multiply_fusion
  (3 shorter events, 0.0 us)
Async XLA Ops:
  0.6 26.6 %copy-start.1 = (f32[3,64,64]{2,1,0:T(8,128)S(1)}, f32[3,64,64]{2,1,0:T(8,128)}, u32[]{:S(2)}) copy-start(f32[3,64,64]{2,1,0:T(8,128)} %param.16) | copy-start | bytes 147460
  24.5 64.7 %all-to-all-start.1 = ((f32[1024,4,128]{2,1,0:T(4,128)}), f32[1024,4,128]{2,1,0:T(4,128)S(1)}, u32[]{:S(2)}, u32[]{:S(2)}) async-start(f32[1024,4,128]{2,1,0:T(4,128)} %get-tuple-element.12), calls=%async_computation.1 | async-start | bytes 4194304 | tf_op jit(solution)/shard_map/all_to_all | solution.py:612
  87.0 21.1 %copy-start.3 = (f32[8,128]{1,0:T(8,128)S(1)}, f32[8,128]{1,0:T(8,128)}, u32[]{:S(2)}) copy-start(f32[8,128]{1,0:T(8,128)} %get-tuple-element.14) | copy-start | bytes 12292
  89.2 1.3 copy-start
  153.3 12.3 %copy-start.2 = (f32[2,8,128]{2,1,0:T(8,128)S(1)}, f32[2,8,128]{2,1,0:T(8,128)}, u32[]{:S(2)}) copy-start(f32[2,8,128]{2,1,0:T(8,128)} %get-tuple-element.17) | copy-start | bytes 24580
  153.3 12.4 %copy-start.4 = (f32[2]{0:T(128)S(1)}, f32[2]{0:T(128)}, u32[]{:S(2)}) copy-start(f32[2]{0:T(128)} %constant.11) | copy-start | bytes 28

commit v3 on v2

--- a/solution.py
+++ b/solution.py
@@ -111,45 +111,51 @@
 
 
 def north_filter(slab_ref, kernel_ref, f, y0, kb):
-    u = slab_ref[f, pl.ds(y0, 24), pl.ds(kb, 8), :]
+    u = slab_ref[pl.ds(y0, 24), pl.ds(kb, 8), :]
     total = kernel_ref[f, 0] * u[8:16]
     for d in range(1, 9):
         total = total + kernel_ref[f, d] * (u[8 - d : 16 - d] + u[8 + d : 16 + d])
     return total
 
 
+def mix_levels(parts, pair):
+    high, low = split(pair)
+    both = jnp.dot(parts, jnp.concatenate([high, low], axis=0), preferred_element_type=F32)
+    half = both.shape[0] // 2
+    return both[:half] + both[half:]
+
+
 def fold_rows(x):
     return jnp.sum(x.reshape(-1, 8, 128), axis=0)
 
 
-def rows_kernel(most, owner, level, row, azimuth, inn, wt, out, labels, count):
+def rows_kernel(most, owner, level, row, azimuth, inn, wt, out, count):
     rows = owner.shape[0]
     tiles = count.shape[0]
     out[...] = jnp.zeros_like(out)
+    lane = lax.broadcasted_iota(jnp.int32, (4, 128), 1)
+    part = lax.broadcasted_iota(jnp.int32, (4, 128), 0)
 
     def clear(t, carry):
         count[t] = 0
-        for j in range(3 * most):
-            labels[t * 3 * most + j] = 0
         return carry
 
     lax.fori_loop(0, tiles, clear, 0)
 
     def one(i, carry):
-        for j in range(4):
-            r = i * 4 + j
+        for j in range(8):
+            r = i * 8 + j
             o = owner[r]
             rank = count[o]
             count[o] = rank + 1
-            slot = o * most + rank
-            labels[slot * 3] = level[r]
-            labels[slot * 3 + 1] = row[r]
-            labels[slot * 3 + 2] = azimuth[r]
-            out[slot, 0:2] = inn[r]
-            out[slot, 2:4] = wt[r]
-        return carry
-
-    lax.fori_loop(0, rows // 4, one, 0)
+            base = o * (most + 1)
+            label = jnp.where(part == 0, level[r], jnp.where(part == 1, row[r], azimuth[r]))
+            out[base + most] = jnp.where(lane == rank, label.astype(F32), out[base + most])
+            out[base + rank, 0:2] = inn[r]
+            out[base + rank, 2:4] = wt[r]
+        return carry
+
+    lax.fori_loop(0, rows // 8, one, 0)
 
 
 def pack_rows(owner, level, row, azimuth, inn, wt, tiles, most):
@@ -157,12 +163,9 @@
     vmem = pl.BlockSpec(memory_space=pltpu.VMEM)
     return pl.pallas_call(
         functools.partial(rows_kernel, most),
-        out_shape=(
-            jax.ShapeDtypeStruct((tiles * most, 4, 128), F32),
-            jax.ShapeDtypeStruct((tiles * 3 * most,), jnp.int32),
-        ),
+        out_shape=jax.ShapeDtypeStruct((tiles * (most + 1), 4, 128), F32),
         in_specs=[smem] * 4 + [vmem] * 2,
-        out_specs=(vmem, smem),
+        out_specs=vmem,
         scratch_shapes=[pltpu.SMEM((tiles,), jnp.int32)],
         compiler_params=params(),
         name="pack_rows",
@@ -182,10 +185,10 @@
 
 def sweep_kernel(
     nx, ny, first, x_ref, east, north, extra, extra2, out, total_out,
-    xbuf, right, left, low, high, slab, flat, fill_sems, sems, parts, sum_sems,
+    xbuf, mid, fbuf, right, left, low, high, fill_sems, sems, parts, sum_sems,
 ):
-    fields, a, b, w = x_ref.shape
-    ys, ks = slab.shape[1] - 16, slab.shape[2]
+    fields, _, _, w = x_ref.shape
+    ys, ks = out.shape[1], out.shape[2]
     ix = lax.axis_index("gx")
     iy = lax.axis_index("gy")
     up_x, down_x = jnp.minimum(ix + 1, nx - 1), jnp.maximum(ix - 1, 0)
@@ -193,8 +196,15 @@
     has_up_x, has_down_x = ix < nx - 1, ix > 0
     has_up_y, has_down_y = iy < ny - 1, iy > 0
 
+    def north_rows(ref, f, start, size):
+        if first:
+            return ref.at[f, :, pl.ds(start, size)]
+        return ref.at[f, pl.ds(start, size)]
+
     def fill(f):
-        return pltpu.make_async_copy(x_ref.at[f], xbuf.at[f], fill_sems.at[f])
+        return pltpu.make_async_copy(
+            x_ref.at[f], north_rows(xbuf, f, 8, ys), fill_sems.at[f]
+        )
 
     for f in range(fields):
         fill(f).start()
@@ -238,11 +248,15 @@
 
     @pl.when(jnp.logical_not(has_down_y))
     def _():
-        slab[:, 0:8] = jnp.zeros((fields, 8, ks, w), F32)
+        for f in range(fields):
+            edge = north_rows(xbuf, f, 0, 8)
+            edge[...] = jnp.zeros(edge.shape, F32)
 
     @pl.when(jnp.logical_not(has_up_y))
     def _():
-        slab[:, ys + 8 :] = jnp.zeros((fields, 8, ks, w), F32)
+        for f in range(fields):
+            edge = north_rows(xbuf, f, ys + 8, 8)
+            edge[...] = jnp.zeros(edge.shape, F32)
 
     def to_up_x(f):
         return send(right, low, sems, 0, f, "gx", up_x)
@@ -252,8 +266,8 @@
 
     def edge_copy(f, which, src, dst, target):
         return pltpu.make_async_remote_copy(
-            src_ref=slab.at[f, pl.ds(src, 8)],
-            dst_ref=slab.at[f, pl.ds(dst, 8)],
+            src_ref=north_rows(x_ref, f, src, 8),
+            dst_ref=north_rows(xbuf, f, dst, 8),
             send_sem=sems.at[0, which, f],
             recv_sem=sems.at[1, which, f],
             device_id={"gy": target},
@@ -261,10 +275,23 @@
         )
 
     def to_up_y(f):
-        return edge_copy(f, 2, ys, 0, up_y)
+        return edge_copy(f, 2, ys - 8, 0, up_y)
 
     def to_down_y(f):
-        return edge_copy(f, 3, 8, ys + 8, down_y)
+        return edge_copy(f, 3, 0, ys + 8, down_y)
+
+    def start_north(f, carry):
+        @pl.when(has_up_y)
+        def _():
+            to_up_y(f).start()
+
+        @pl.when(has_down_y)
+        def _():
+            to_down_y(f).start()
+
+        return carry
+
+    lax.fori_loop(0, fields, start_north, 0)
 
     def share(axis, n, slot, peer, row):
         return pltpu.make_async_remote_copy(
@@ -291,36 +318,19 @@
         for j in range(1, nx):
             share("gx", nx, ix, lax.rem(ix + j, nx), 0).start()
 
-    def pack(f, carry):
+    def fill_wait(f, carry):
         fill(f).wait()
-
-        def put_right(g, v):
-            right[f, g] = v
-
-        def put_left(g, v):
-            left[f, g] = v
-
-        pack_rims(lambda s: xbuf[f, s], put_right, put_left, a // 16, b)
-
-        @pl.when(has_up_x)
-        def _():
-            to_up_x(f).start()
-
-        @pl.when(has_down_x)
-        def _():
-            to_down_x(f).start()
-
-        return carry
-
-    lax.fori_loop(0, fields, pack, 0)
+        return carry
+
+    lax.fori_loop(0, fields, fill_wait, 0)
 
     if first:
 
         def square(i, total):
-            v = xbuf[i // a, i % a]
+            v = xbuf[i // ks, i % ks, pl.ds(8, ys)]
             return total + fold_rows(v * v)
 
-        total_out[...] = lax.fori_loop(0, fields * a, square, jnp.zeros((8, w), F32))
+        total_out[...] = lax.fori_loop(0, fields * ks, square, jnp.zeros((8, w), F32))
     else:
         for j in range(1, nx):
             arrival("gx", lax.rem(ix + j, nx), 0).wait_recv()
@@ -331,83 +341,87 @@
         for j in range(1, ny):
             share("gy", ny, iy, lax.rem(iy + j, ny), 1).start()
 
-    def middle(f, carry):
-        @pl.when(has_down_x)
-        def _():
-            to_up_x(f).wait_recv()
-
-        @pl.when(has_up_x)
-        def _():
-            to_down_x(f).wait_recv()
+    def stage_north(f, carry):
+        @pl.when(has_down_y)
+        def _():
+            to_up_y(f).wait_recv()
+
+        @pl.when(has_up_y)
+        def _():
+            to_down_y(f).wait_recv()
 
         if first:
-            pitch = b + 8
-
-            def put(s, v):
-                flat[pl.ds(pl.multiple_of(s * pitch, 8), b), :] = v
-
-            east_filter(lambda s: xbuf[f, s], low, high, put, east, f, a // 16, b)
+            pitch = ys + 16
+            rows_of = xbuf.reshape(fields * ks * pitch, w)
             v = extra[f]
 
             def one(p, carry):
                 for j in range(4):
                     y = p * 8 + 2 * j
+                    at = f * (ks * pitch) + y
                     x = jnp.concatenate(
-                        [flat[pl.ds(y, a, stride=pitch), :], flat[pl.ds(y + 1, a, stride=pitch), :]],
+                        [
+                            rows_of[pl.ds(at, ks, stride=pitch), :],
+                            rows_of[pl.ds(at + 1, ks, stride=pitch), :],
+                        ],
                         axis=1,
                     )
-                    h, l = split(x)
-                    r = jnp.dot(
-                        v, jnp.concatenate([h, l, h, l], axis=0), preferred_element_type=F32
-                    )
-                    slab[f, 8 + y] = r[:, :w]
-                    slab[f, 9 + y] = r[:, w:]
+                    r = mix_levels(v, x)
+                    mid[y] = r[:, :w]
+                    mid[y + 1] = r[:, w:]
                 return carry
 
-            lax.fori_loop(0, b // 8, one, 0)
+            lax.fori_loop(0, pitch // 8, one, 0)
+            slab = mid
         else:
-
-            def put_slab(s, v):
-                slab[f, 8 + s] = v
-
-            east_filter(lambda s: xbuf[f, s], low, high, put_slab, east, f, a // 16, b)
-
-        @pl.when(has_up_y)
-        def _():
-            to_up_y(f).start()
-
-        @pl.when(has_down_y)
-        def _():
-            to_down_y(f).start()
-
-        return carry
-
-    lax.fori_loop(0, fields, middle, 0)
-
-    def last(f, carry):
-        @pl.when(has_down_y)
-        def _():
-            to_up_y(f).wait_recv()
-
-        @pl.when(has_up_y)
-        def _():
-            to_down_y(f).wait_recv()
-
-        def one(i, carry):
+            slab = xbuf.at[f]
+
+        def two(i, carry):
             y0 = (i // (ks // 8)) * 8
             kb = pl.multiple_of((i % (ks // 8)) * 8, 8)
-            total = north_filter(slab, north, f, y0, kb)
-            for j in range(8):
-                value = total[j]
-                if first:
-                    value = value * extra2[f, pl.ds(y0 + j, 1), :]
-                out[f, y0 + j, pl.ds(kb, 8), :] = value
+            fbuf[f, pl.ds(y0, 8), pl.ds(kb, 8), :] = north_filter(slab, north, f, y0, kb)
             return carry
 
-        lax.fori_loop(0, (ys // 8) * (ks // 8), one, 0)
-        return carry
-
-    lax.fori_loop(0, fields, last, 0)
+        lax.fori_loop(0, (ys // 8) * (ks // 8), two, 0)
+
+        def put_right(g, v):
+            right[f, g] = v
+
+        def put_left(g, v):
+            left[f, g] = v
+
+        pack_rims(lambda s: fbuf[f, s], put_right, put_left, ys // 16, ks)
+
+        @pl.when(has_up_x)
+        def _():
+            to_up_x(f).start()
+
+        @pl.when(has_down_x)
+        def _():
+            to_down_x(f).start()
+
+        return carry
+
+    lax.fori_loop(0, fields, stage_north, 0)
+
+    def stage_east(f, carry):
+        @pl.when(has_down_x)
+        def _():
+            to_up_x(f).wait_recv()
+
+        @pl.when(has_up_x)
+        def _():
+            to_down_x(f).wait_recv()
+
+        def put(s, v):
+            if first:
+                v = v * extra2[f, pl.ds(s, 1), :]
+            out[f, s] = v
+
+        east_filter(lambda s: fbuf[f, s], low, high, put, east, f, ys // 16, ks)
+        return carry
+
+    lax.fori_loop(0, fields, stage_east, 0)
 
     if not first:
         for j in range(1, ny):
@@ -449,8 +463,9 @@
     ys, ks = (b, a) if first else (a, b)
     smem = pl.BlockSpec(memory_space=pltpu.SMEM)
     vmem = pl.BlockSpec(memory_space=pltpu.VMEM)
-    rim = pltpu.VMEM((f, a // 16, b, w), F32)
+    rim = pltpu.VMEM((f, ys // 16, ks, w), F32)
     total = (8, w) if first else (2, 8, w)
+    wide = (f, a, b + 16, w) if first else (f, a + 16, b, w)
     return pl.pallas_call(
         functools.partial(sweep_kernel, nx, ny, first),
         in_specs=[pl.BlockSpec(memory_space=pl.ANY), smem, smem, vmem, vmem],
@@ -460,13 +475,13 @@
             jax.ShapeDtypeStruct(total, F32),
         ),
         scratch_shapes=[
-            pltpu.VMEM((f, a, b, w), F32),
+            pltpu.VMEM(wide, F32),
+            pltpu.VMEM((ys + 16, ks, w), F32),
+            pltpu.VMEM((f, ys, ks, w), F32),
             rim,
             rim,
             rim,
             rim,
-            pltpu.VMEM((f, ys + 16, ks, w), F32),
-            pltpu.VMEM((a * (b + 8), w), F32),
             pltpu.SemaphoreType.DMA((f,)),
             pltpu.SemaphoreType.DMA((2, 4, f)),
             pltpu.VMEM((2, max(nx, ny), 2, 8, w), F32),
@@ -482,7 +497,7 @@
 
 
 def observe_kernel(
-    cell, cosine, sine, s_ref, spread, rows_ref, adj, obs, a0, a1, a2, m0, m1
+    most, cell, cosine, sine, s_ref, spread, rows_ref, adj, obs, a0, a1, a2, m0, m1
 ):
     fields, b, w = spread.shape
     a = s_ref.shape[1] // b
@@ -491,7 +506,7 @@
     for f in range(fields):
         adjs[f][...] = jnp.zeros_like(a0)
 
-    count = rows_ref.shape[0]
+    count = cell.shape[0]
 
     def pick(i, carry):
         for j in range(8):
@@ -505,10 +520,12 @@
 
     def weigh(i, total):
         at = pl.ds(pl.multiple_of(i * 8, 8), 8)
-        d0 = m0[at, :] - rows_ref[at, 0, :]
-        d1 = m1[at, :] - rows_ref[at, 1, :]
-        w0 = rows_ref[at, 2, :] * d0
-        w1 = rows_ref[at, 3, :] * d1
+        first = (i * 8 // most) * (most + 1) + (i * 8) % most
+        slot = pl.ds(first, 8)
+        d0 = m0[at, :] - rows_ref[slot, 0, :]
+        d1 = m1[at, :] - rows_ref[slot, 1, :]
+        w0 = rows_ref[slot, 2, :] * d0
+        w1 = rows_ref[slot, 3, :] * d1
         m0[at, :] = w0
         m1[at, :] = w1
         return total + (w0 * d0 + w1 * d1)
@@ -537,13 +554,13 @@
         lax.fori_loop(0, b, scale_rows, 0)
 
 
-def observe(cell, cosine, sine, state, spread, rows):
+def observe(cell, cosine, sine, state, spread, rows, most):
     f, b, w = spread.shape
     cells = state.shape[1]
     smem = pl.BlockSpec(memory_space=pltpu.SMEM)
     vmem = pl.BlockSpec(memory_space=pltpu.VMEM)
     return pl.pallas_call(
-        observe_kernel,
+        functools.partial(observe_kernel, most),
         in_specs=[smem] * 3 + [vmem] * 3,
         out_specs=(vmem, vmem),
         out_shape=(
@@ -551,7 +568,7 @@
             jax.ShapeDtypeStruct((8, w), F32),
         ),
         scratch_shapes=[pltpu.VMEM((cells, w), F32)] * 3
-        + [pltpu.VMEM((rows.shape[0], w), F32)] * 2,
+        + [pltpu.VMEM((cell.shape[0], w), F32)] * 2,
         compiler_params=params(),
         name="observe",
     )(cell, cosine, sine, state, spread, rows)
@@ -563,8 +580,7 @@
     v = vert[0]
     for j in range(b // 2):
         x = jnp.concatenate([x_ref[0, 2 * j], x_ref[0, 2 * j + 1]], axis=1)
-        h, l = split(x)
-        r = jnp.dot(v, jnp.concatenate([h, l, h, l], axis=0), preferred_element_type=F32)
+        r = mix_levels(v, x)
         flat[pl.ds(2 * j, a, stride=pitch), :] = r[:, :w]
         flat[pl.ds(2 * j + 1, a, stride=pitch), :] = r[:, w:]
     for s in range(a):
@@ -580,7 +596,7 @@
         grid=(f, b // rows),
         in_specs=[
             pl.BlockSpec((1, rows, a, w), lambda i, j: (i, j, 0, 0)),
-            pl.BlockSpec((1, a, 4 * a), lambda i, j: (i, 0, 0)),
+            pl.BlockSpec((1, 2 * a, 2 * a), lambda i, j: (i, 0, 0)),
             tall,
         ],
         out_specs=tall,
@@ -594,7 +610,8 @@
 def vertical_parts(v):
     high = lax.reduce_precision(v, 8, 7)
     low = lax.reduce_precision(v - high, 8, 7)
-    return jnp.concatenate([high, high, low, low], axis=2).astype(BF16)
+    both = jnp.concatenate([high, low], axis=1)
+    return jnp.concatenate([both, both], axis=2).astype(BF16)
 
 
 def body(
@@ -606,18 +623,16 @@
     levels = control.shape[1]
     axes = ("gx", "gy")
 
-    rows, labels = pack_rows(
+    rows = pack_rows(
         tile_owner, gate_level, tile_row, beam_azimuth, innovation, obs_weight, tiles, most
     )
     rows = lax.all_to_all(rows, axes, split_axis=0, concat_axis=0, tiled=True)
-    labels = lax.all_to_all(
-        labels.reshape(tiles * most, 3), axes, split_axis=0, concat_axis=0, tiled=True
-    )
+    labels = rows.reshape(tiles, most + 1, 4, -1)[:, most, :3, :most]
     vert = vertical_parts(vertical)
     vert_back = vertical_parts(jnp.swapaxes(vertical, 1, 2))
     state, square = sweep(True, control, kernel_east, kernel_north, vert, spread)
-    cell = labels[:, 1] * levels + labels[:, 0]
-    angle = labels[:, 2].astype(F32) * (2.0 * math.pi / 360.0)
+    cell = (labels[:, 1] * levels + labels[:, 0]).astype(jnp.int32).reshape(-1)
+    angle = labels[:, 2].reshape(-1) * (2.0 * math.pi / 360.0)
     adj, obs = observe(
         cell,
         jnp.cos(angle),
@@ -625,6 +640,7 @@
         state.reshape(state.shape[0], -1, state.shape[3]),
         spread,
         rows,
+        most,
     )
     parts = jnp.stack([square, obs])
     smooth, totals = sweep(False, adj, kernel_east, kernel_north, parts, spread)

time: 169 us -> 171 us (1.012)
  Pallas kernels: 141 us -> 156 us
  blocking collectives: 14.6 us -> 0 us
  starting transfers between devices: 2.73 us -> 7.3 us
    pallas_call x2, Pallas kernels: 103 us -> 118 us  [sweep(): pl.pallas_call(functools.partial(sweep_kernel, nx, ny, first), in_specs=[...]
    all_to_all x1 -> x0, blocking collectives: 14.6 us -> none  [body(): lax.all_to_all(labels.reshape(tiles * most, 3), axes, split_axis=0, conca...]
    all_to_all x1, starting transfers between devices: 2.73 us -> 7.3 us  [body(): rows = lax.all_to_all(rows, axes, split_axis=0, concat_axis=0, tiled=True)]
  transfers between devices with their start and end apart: 1 -> 1, of which waited for: 0 -> 0; matrix products, arithmetic and copies ran while one was open for 2% -> 1% of each run, Pallas kernels for 35% -> 42%
where the time goes in v3:
time: 171 us; the launch traced here: 170 us
  Pallas kernels  156 us (91%)
  starting transfers between devices  7.3 us (4%)
  other arithmetic  4.07 us (2%)
  local copies, waits for them, and re-layouts  2.11 us (1%)
    pallas_call x2, Pallas kernels, sweep(): pl.pallas_call(functools.partial(sweep_kernel, nx, ny, first), in_specs=[...  118 us
    pallas_call x1, Pallas kernels, observe(): pl.pallas_call(functools.partial(observe_kernel, most), in_specs=[smem] *...  19.5 us
    pallas_call x1, Pallas kernels, gradient_of(): pl.pallas_call(gradient_kernel, grid=(f, b // rows), in_specs=[pl.BlockSp...  12.2 us
    all_to_all x1, starting transfers between devices, body(): rows = lax.all_to_all(rows, axes, split_axis=0, concat_axis=0, tiled=True)  7.3 us
    pallas_call x1, Pallas kernels, pack_rows(): pl.pallas_call(functools.partial(rows_kernel, most), out_shape=jax.ShapeD...  5.89 us
  transfers between devices with their start and end apart: 1, of which 0 were waited for; matrix products, arithmetic and copies ran while one was open for 1% of the time, Pallas kernels for 42%

profile of v3, /device:TPU:0, one launch (start us, length us, event | category | flops | bytes accessed | tf_op | source)
XLA Modules:
  0.0 169.9 jit_solution(6743827177747860531)
XLA Ops:
  0.6 0.0 copy-start.1
  0.6 5.9 %pack_rows.1 = f32[1056,4,128]{2,1,0:T(4,128)} custom-call(s32[512]{0:T(512)} %owner.1, s32[512]{0:T(512)} %level.1, s32[512]{0:T(512)} %row.1, s32[512]{0:T(512)} %azimuth.1, f32[512,2,128]{2,1,0:T(2,128)} %inn.1, f32[512,2,128]{2,1,0:T(2,128)} %wt.1), custom_call_target="tpu_custom_call" | custom-call | tf_op jit(solution)/shard_map/pack_rows/pallas_call | solution.py:164
  6.5 7.3 %all-to-all-start = ((f32[1056,4,128]{2,1,0:T(4,128)}), f32[1056,4,128]{2,1,0:T(4,128)S(1)}, u32[]{:S(2)}, u32[]{:S(2)}) async-start(f32[1056,4,128]{2,1,0:T(4,128)} %pack_rows.1), calls=%async_computation | async-start | bytes 4325376 | tf_op jit(solution)/shard_map/all_to_all | solution.py:629
  13.8 0.0 copy-done.1
  13.9 0.1 copy.14
  14.0 0.7 pad_maximum_fusion.extra
  14.7 70.7 %sweep_forward.1 = (f32[3,64,64,128]{3,2,1,0:T(8,128)}, f32[8,128]{1,0:T(8,128)}) custom-call(f32[3,64,64,128]{3,2,1,0:T(8,128)} %c_ref.1, f32[3,9]{1,0:T(4,128)} %east.3, f32[3,9]{1,0:T(4,128)} %north.3, bf16[3,128,128]{2,1,0:T(8,128)(2,1)} %pad_maximum_fusion.extra, f32[3,64,128]{2,1,0:T(8,128)} %extra2.3), custom_call_target="tpu_custom_call" | custom-call | tf_op jit(solution)/shard_map/sweep_forward/pallas_call | solution.py:469
  85.5 0.0 copy-start.3
  85.6 0.7 pad_maximum_fusion.1.vert
  86.3 0.0 all-to-all-done.rows_ref
  86.3 0.0 copy-start
  86.3 0.6 sine_reduce_fusion
  86.9 0.1 fusion.2
  87.0 0.7 cos.6.cosine
  87.6 0.7 sin.6.sine
  88.3 0.7 convert_element_type.10.cell
  88.9 0.0 copy-done
  88.9 19.5 %observe.1 = (f32[3,64,64,128]{3,2,1,0:T(8,128)}, f32[8,128]{1,0:T(8,128)}) custom-call(s32[1024]{0:T(1024)} %convert_element_type.10.cell, f32[1024]{0:T(1024)} %cos.6.cosine, f32[1024]{0:T(1024)} %sin.6.sine, f32[3,4096,128]{2,1,0:T(8,128)} %bitcast.14, f32[3,64,128]{2,1,0:T(8,128)} %extra2.3, f32[1056,4,128]{2,1,0:T(4,128)} %copy-done), custom_call_target="tpu_custom_call" | custom-call | tf_op jit(solution)/shard_map/observe/pallas_call | solution.py:562
  108.4 0.0 copy-done.3
  108.4 1.3 pad_maximum_fusion.2.extra
  109.7 47.4 %sweep_back.1 = (f32[3,64,64,128]{3,2,1,0:T(8,128)}, f32[2,8,128]{2,1,0:T(8,128)}) custom-call(f32[3,64,64,128]{3,2,1,0:T(8,128)} %get-tuple-element.9.x_ref, f32[3,9]{1,0:T(4,128)} %east.3, f32[3,9]{1,0:T(4,128)} %north.3, f32[2,8,128]{2,1,0:T(8,128)} %pad_maximum_fusion.2.extra, f32[3,64,128]{2,1,0:T(8,128)} %extra2.3), custom_call_target="tpu_custom_call" | custom-call | tf_op jit(solution)/shard_map/sweep_back/pallas_call | solution.py:469
  157.1 0.0 copy-start.2
  157.1 0.0 copy-start.4
  157.1 12.2 %gradient.1 = f32[3,64,64,128]{3,2,1,0:T(8,128)} custom-call(f32[3,64,64,128]{3,2,1,0:T(8,128)} %get-tuple-element.12.x_ref, bf16[3,128,128]{2,1,0:T(8,128)(2,1)} %pad_maximum_fusion.1.vert, f32[3,64,64,128]{3,2,1,0:T(8,128)} %c_ref.1), custom_call_target="tpu_custom_call" | custom-call | tf_op jit(solution)/shard_map/gradient/pallas_call | solution.py:594
  169.3 0.0 copy-done.2
  169.3 0.1 reduce_sum.9
  169.4 0.0 copy-done.4
  169.4 0.5 multiply_multiply_fusion
  (5 shorter events, 0.1 us)
Async XLA Ops:
  0.6 13.2 %copy-start.1 = (f32[3,64,64]{2,1,0:T(8,128)S(1)}, f32[3,64,64]{2,1,0:T(8,128)}, u32[]{:S(2)}) copy-start(f32[3,64,64]{2,1,0:T(8,128)} %param.16) | copy-start | bytes 147460
  6.5 79.8 %all-to-all-start = ((f32[1056,4,128]{2,1,0:T(4,128)}), f32[1056,4,128]{2,1,0:T(4,128)S(1)}, u32[]{:S(2)}, u32[]{:S(2)}) async-start(f32[1056,4,128]{2,1,0:T(4,128)} %pack_rows.1), calls=%async_computation | async-start | bytes 4325376 | tf_op jit(solution)/shard_map/all_to_all | solution.py:629
  85.5 22.9 %copy-start.3 = (f32[8,128]{1,0:T(8,128)S(1)}, f32[8,128]{1,0:T(8,128)}, u32[]{:S(2)}) copy-start(f32[8,128]{1,0:T(8,128)} %get-tuple-element.10) | copy-start | bytes 12292
  86.3 2.6 %copy-start = (f32[1056,4,128]{2,1,0:T(4,128)}, f32[1056,4,128]{2,1,0:T(4,128)S(1)}, u32[]{:S(2)}) copy-start(f32[1056,4,128]{2,1,0:T(4,128)S(1)} %all-to-all-done.rows_ref) | copy-start | bytes 6488068
  157.1 12.3 %copy-start.2 = (f32[2,8,128]{2,1,0:T(8,128)S(1)}, f32[2,8,128]{2,1,0:T(8,128)}, u32[]{:S(2)}) copy-start(f32[2,8,128]{2,1,0:T(8,128)} %get-tuple-element.13) | copy-start | bytes 24580
  157.1 12.4 %copy-start.4 = (f32[2]{0:T(128)S(1)}, f32[2]{0:T(128)}, u32[]{:S(2)}) copy-start(f32[2]{0:T(128)} %constant.11) | copy-start | bytes 28

commit v4 on v2

--- a/solution.py
+++ b/solution.py
@@ -118,38 +118,44 @@
     return total
 
 
+def mix_levels(parts, pair):
+    high, low = split(pair)
+    both = jnp.dot(parts, jnp.concatenate([high, low], axis=0), preferred_element_type=F32)
+    half = both.shape[0] // 2
+    return both[:half] + both[half:]
+
+
 def fold_rows(x):
     return jnp.sum(x.reshape(-1, 8, 128), axis=0)
 
 
-def rows_kernel(most, owner, level, row, azimuth, inn, wt, out, labels, count):
+def rows_kernel(most, owner, level, row, azimuth, inn, wt, out, count):
     rows = owner.shape[0]
     tiles = count.shape[0]
     out[...] = jnp.zeros_like(out)
+    lane = lax.broadcasted_iota(jnp.int32, (4, 128), 1)
+    part = lax.broadcasted_iota(jnp.int32, (4, 128), 0)
 
     def clear(t, carry):
         count[t] = 0
-        for j in range(3 * most):
-            labels[t * 3 * most + j] = 0
         return carry
 
     lax.fori_loop(0, tiles, clear, 0)
 
     def one(i, carry):
-        for j in range(4):
-            r = i * 4 + j
+        for j in range(8):
+            r = i * 8 + j
             o = owner[r]
             rank = count[o]
             count[o] = rank + 1
-            slot = o * most + rank
-            labels[slot * 3] = level[r]
-            labels[slot * 3 + 1] = row[r]
-            labels[slot * 3 + 2] = azimuth[r]
-            out[slot, 0:2] = inn[r]
-            out[slot, 2:4] = wt[r]
-        return carry
-
-    lax.fori_loop(0, rows // 4, one, 0)
+            base = o * (most + 1)
+            label = jnp.where(part == 0, level[r], jnp.where(part == 1, row[r], azimuth[r]))
+            out[base + most] = jnp.where(lane == rank, label.astype(F32), out[base + most])
+            out[base + rank, 0:2] = inn[r]
+            out[base + rank, 2:4] = wt[r]
+        return carry
+
+    lax.fori_loop(0, rows // 8, one, 0)
 
 
 def pack_rows(owner, level, row, azimuth, inn, wt, tiles, most):
@@ -157,12 +163,9 @@
     vmem = pl.BlockSpec(memory_space=pltpu.VMEM)
     return pl.pallas_call(
         functools.partial(rows_kernel, most),
-        out_shape=(
-            jax.ShapeDtypeStruct((tiles * most, 4, 128), F32),
-            jax.ShapeDtypeStruct((tiles * 3 * most,), jnp.int32),
-        ),
+        out_shape=jax.ShapeDtypeStruct((tiles * (most + 1), 4, 128), F32),
         in_specs=[smem] * 4 + [vmem] * 2,
-        out_specs=(vmem, smem),
+        out_specs=vmem,
         scratch_shapes=[pltpu.SMEM((tiles,), jnp.int32)],
         compiler_params=params(),
         name="pack_rows",
@@ -356,10 +359,7 @@
                         [flat[pl.ds(y, a, stride=pitch), :], flat[pl.ds(y + 1, a, stride=pitch), :]],
                         axis=1,
                     )
-                    h, l = split(x)
-                    r = jnp.dot(
-                        v, jnp.concatenate([h, l, h, l], axis=0), preferred_element_type=F32
-                    )
+                    r = mix_levels(v, x)
                     slab[f, 8 + y] = r[:, :w]
                     slab[f, 9 + y] = r[:, w:]
                 return carry
@@ -482,7 +482,7 @@
 
 
 def observe_kernel(
-    cell, cosine, sine, s_ref, spread, rows_ref, adj, obs, a0, a1, a2, m0, m1
+    most, cell, cosine, sine, s_ref, spread, rows_ref, adj, obs, a0, a1, a2, m0, m1
 ):
     fields, b, w = spread.shape
     a = s_ref.shape[1] // b
@@ -491,7 +491,7 @@
     for f in range(fields):
         adjs[f][...] = jnp.zeros_like(a0)
 
-    count = rows_ref.shape[0]
+    count = cell.shape[0]
 
     def pick(i, carry):
         for j in range(8):
@@ -505,10 +505,12 @@
 
     def weigh(i, total):
         at = pl.ds(pl.multiple_of(i * 8, 8), 8)
-        d0 = m0[at, :] - rows_ref[at, 0, :]
-        d1 = m1[at, :] - rows_ref[at, 1, :]
-        w0 = rows_ref[at, 2, :] * d0
-        w1 = rows_ref[at, 3, :] * d1
+        first = (i * 8 // most) * (most + 1) + (i * 8) % most
+        slot = pl.ds(first, 8)
+        d0 = m0[at, :] - rows_ref[slot, 0, :]
+        d1 = m1[at, :] - rows_ref[slot, 1, :]
+        w0 = rows_ref[slot, 2, :] * d0
+        w1 = rows_ref[slot, 3, :] * d1
         m0[at, :] = w0
         m1[at, :] = w1
         return total + (w0 * d0 + w1 * d1)
@@ -537,13 +539,13 @@
         lax.fori_loop(0, b, scale_rows, 0)
 
 
-def observe(cell, cosine, sine, state, spread, rows):
+def observe(cell, cosine, sine, state, spread, rows, most):
     f, b, w = spread.shape
     cells = state.shape[1]
     smem = pl.BlockSpec(memory_space=pltpu.SMEM)
     vmem = pl.BlockSpec(memory_space=pltpu.VMEM)
     return pl.pallas_call(
-        observe_kernel,
+        functools.partial(observe_kernel, most),
         in_specs=[smem] * 3 + [vmem] * 3,
         out_specs=(vmem, vmem),
         out_shape=(
@@ -551,7 +553,7 @@
             jax.ShapeDtypeStruct((8, w), F32),
         ),
         scratch_shapes=[pltpu.VMEM((cells, w), F32)] * 3
-        + [pltpu.VMEM((rows.shape[0], w), F32)] * 2,
+        + [pltpu.VMEM((cell.shape[0], w), F32)] * 2,
         compiler_params=params(),
         name="observe",
     )(cell, cosine, sine, state, spread, rows)
@@ -563,8 +565,7 @@
     v = vert[0]
     for j in range(b // 2):
         x = jnp.concatenate([x_ref[0, 2 * j], x_ref[0, 2 * j + 1]], axis=1)
-        h, l = split(x)
-        r = jnp.dot(v, jnp.concatenate([h, l, h, l], axis=0), preferred_element_type=F32)
+        r = mix_levels(v, x)
         flat[pl.ds(2 * j, a, stride=pitch), :] = r[:, :w]
         flat[pl.ds(2 * j + 1, a, stride=pitch), :] = r[:, w:]
     for s in range(a):
@@ -580,7 +581,7 @@
         grid=(f, b // rows),
         in_specs=[
             pl.BlockSpec((1, rows, a, w), lambda i, j: (i, j, 0, 0)),
-            pl.BlockSpec((1, a, 4 * a), lambda i, j: (i, 0, 0)),
+            pl.BlockSpec((1, 2 * a, 2 * a), lambda i, j: (i, 0, 0)),
             tall,
         ],
         out_specs=tall,
@@ -594,7 +595,8 @@
 def vertical_parts(v):
     high = lax.reduce_precision(v, 8, 7)
     low = lax.reduce_precision(v - high, 8, 7)
-    return jnp.concatenate([high, high, low, low], axis=2).astype(BF16)
+    both = jnp.concatenate([high, low], axis=1)
+    return jnp.concatenate([both, both], axis=2).astype(BF16)
 
 
 def body(
@@ -606,18 +608,16 @@
     levels = control.shape[1]
     axes = ("gx", "gy")
 
-    rows, labels = pack_rows(
+    rows = pack_rows(
         tile_owner, gate_level, tile_row, beam_azimuth, innovation, obs_weight, tiles, most
     )
     rows = lax.all_to_all(rows, axes, split_axis=0, concat_axis=0, tiled=True)
-    labels = lax.all_to_all(
-        labels.reshape(tiles * most, 3), axes, split_axis=0, concat_axis=0, tiled=True
-    )
+    labels = rows.reshape(tiles, most + 1, 4, -1)[:, most, :3, :most]
     vert = vertical_parts(vertical)
     vert_back = vertical_parts(jnp.swapaxes(vertical, 1, 2))
     state, square = sweep(True, control, kernel_east, kernel_north, vert, spread)
-    cell = labels[:, 1] * levels + labels[:, 0]
-    angle = labels[:, 2].astype(F32) * (2.0 * math.pi / 360.0)
+    cell = (labels[:, 1] * levels + labels[:, 0]).astype(jnp.int32).reshape(-1)
+    angle = labels[:, 2].reshape(-1) * (2.0 * math.pi / 360.0)
     adj, obs = observe(
         cell,
         jnp.cos(angle),
@@ -625,6 +625,7 @@
         state.reshape(state.shape[0], -1, state.shape[3]),
         spread,
         rows,
+        most,
     )
     parts = jnp.stack([square, obs])
     smooth, totals = sweep(False, adj, kernel_east, kernel_north, parts, spread)

time: 169 us -> 158 us (0.935)
  blocking collectives: 14.6 us -> 0 us
  starting transfers between devices: 2.73 us -> 7.3 us
    all_to_all x1 -> x0, blocking collectives: 14.6 us -> none  [body(): lax.all_to_all(labels.reshape(tiles * most, 3), axes, split_axis=0, conca...]
    all_to_all x1, starting transfers between devices: 2.73 us -> 7.3 us  [body(): rows = lax.all_to_all(rows, axes, split_axis=0, concat_axis=0, tiled=True)]
  transfers between devices with their start and end apart: 1 -> 1, of which waited for: 0 -> 0; matrix products, arithmetic and copies ran while one was open for 2% -> 1% of each run, Pallas kernels for 35% -> 39%
where the time goes in v4:
time: 158 us; the launch traced here: 155 us
  Pallas kernels  141 us (89%)
  starting transfers between devices  7.3 us (5%)
  other arithmetic  4.07 us (3%)
  local copies, waits for them, and re-layouts  2.11 us (1%)
    pallas_call x2, Pallas kernels, sweep(): pl.pallas_call(functools.partial(sweep_kernel, nx, ny, first), in_specs=[...  103 us
    pallas_call x1, Pallas kernels, observe(): pl.pallas_call(functools.partial(observe_kernel, most), in_specs=[smem] *...  19.7 us
    pallas_call x1, Pallas kernels, gradient_of(): pl.pallas_call(gradient_kernel, grid=(f, b // rows), in_specs=[pl.BlockSp...  12.2 us
    all_to_all x1, starting transfers between devices, body(): rows = lax.all_to_all(rows, axes, split_axis=0, concat_axis=0, tiled=True)  7.3 us
    pallas_call x1, Pallas kernels, pack_rows(): pl.pallas_call(functools.partial(rows_kernel, most), out_shape=jax.ShapeD...  5.89 us
  transfers between devices with their start and end apart: 1, of which 0 were waited for; matrix products, arithmetic and copies ran while one was open for 1% of the time, Pallas kernels for 39%

profile of v4, /device:TPU:0, one launch (start us, length us, event | category | flops | bytes accessed | tf_op | source)
XLA Modules:
  0.0 155.3 jit_solution(15933478632005168283)
XLA Ops:
  0.6 0.0 copy-start.1
  0.6 5.9 %pack_rows.1 = f32[1056,4,128]{2,1,0:T(4,128)} custom-call(s32[512]{0:T(512)} %owner.1, s32[512]{0:T(512)} %level.1, s32[512]{0:T(512)} %row.1, s32[512]{0:T(512)} %azimuth.1, f32[512,2,128]{2,1,0:T(2,128)} %inn.1, f32[512,2,128]{2,1,0:T(2,128)} %wt.1), custom_call_target="tpu_custom_call" | custom-call | tf_op jit(solution)/shard_map/pack_rows/pallas_call | solution.py:164
  6.5 7.3 %all-to-all-start = ((f32[1056,4,128]{2,1,0:T(4,128)}), f32[1056,4,128]{2,1,0:T(4,128)S(1)}, u32[]{:S(2)}, u32[]{:S(2)}) async-start(f32[1056,4,128]{2,1,0:T(4,128)} %pack_rows.1), calls=%async_computation | async-start | bytes 4325376 | tf_op jit(solution)/shard_map/all_to_all | solution.py:614
  13.8 0.0 copy-done.1
  13.9 0.1 copy.14
  14.0 0.7 pad_maximum_fusion.extra
  14.7 60.1 %sweep_forward.1 = (f32[3,64,64,128]{3,2,1,0:T(8,128)}, f32[8,128]{1,0:T(8,128)}) custom-call(f32[3,64,64,128]{3,2,1,0:T(8,128)} %c_ref.1, f32[3,9]{1,0:T(4,128)} %east.3, f32[3,9]{1,0:T(4,128)} %north.3, bf16[3,128,128]{2,1,0:T(8,128)(2,1)} %pad_maximum_fusion.extra, f32[3,64,128]{2,1,0:T(8,128)} %extra2.3), custom_call_target="tpu_custom_call" | custom-call | tf_op jit(solution)/shard_map/sweep_forward/pallas_call | solution.py:454
  74.8 0.0 copy-start.3
  74.9 0.7 pad_maximum_fusion.1.vert
  75.7 0.0 all-to-all-done.rows_ref
  75.7 0.0 copy-start
  75.7 0.6 sine_reduce_fusion
  76.2 0.1 fusion.2
  76.3 0.7 cos.6.cosine
  77.0 0.7 sin.6.sine
  77.6 0.7 convert_element_type.10.cell
  78.3 0.0 copy-done
  78.3 19.7 %observe.1 = (f32[3,64,64,128]{3,2,1,0:T(8,128)}, f32[8,128]{1,0:T(8,128)}) custom-call(s32[1024]{0:T(1024)} %convert_element_type.10.cell, f32[1024]{0:T(1024)} %cos.6.cosine, f32[1024]{0:T(1024)} %sin.6.sine, f32[3,4096,128]{2,1,0:T(8,128)} %bitcast.14, f32[3,64,128]{2,1,0:T(8,128)} %extra2.3, f32[1056,4,128]{2,1,0:T(4,128)} %copy-done), custom_call_target="tpu_custom_call" | custom-call | tf_op jit(solution)/shard_map/observe/pallas_call | solution.py:547
  98.0 0.0 copy-done.3
  98.0 1.3 pad_maximum_fusion.2.extra
  99.3 43.2 %sweep_back.1 = (f32[3,64,64,128]{3,2,1,0:T(8,128)}, f32[2,8,128]{2,1,0:T(8,128)}) custom-call(f32[3,64,64,128]{3,2,1,0:T(8,128)} %get-tuple-element.9.x_ref, f32[3,9]{1,0:T(4,128)} %east.3, f32[3,9]{1,0:T(4,128)} %north.3, f32[2,8,128]{2,1,0:T(8,128)} %pad_maximum_fusion.2.extra, f32[3,64,128]{2,1,0:T(8,128)} %extra2.3), custom_call_target="tpu_custom_call" | custom-call | tf_op jit(solution)/shard_map/sweep_back/pallas_call | solution.py:454
  142.4 0.0 copy-start.2
  142.5 0.0 copy-start.4
  142.5 12.2 %gradient.1 = f32[3,64,64,128]{3,2,1,0:T(8,128)} custom-call(f32[3,64,64,128]{3,2,1,0:T(8,128)} %get-tuple-element.12.x_ref, bf16[3,128,128]{2,1,0:T(8,128)(2,1)} %pad_maximum_fusion.1.vert, f32[3,64,64,128]{3,2,1,0:T(8,128)} %c_ref.1), custom_call_target="tpu_custom_call" | custom-call | tf_op jit(solution)/shard_map/gradient/pallas_call | solution.py:579
  154.7 0.0 copy-done.2
  154.7 0.1 reduce_sum.9
  154.8 0.0 copy-done.4
  154.8 0.5 multiply_multiply_fusion
  (5 shorter events, 0.1 us)
Async XLA Ops:
  0.6 13.2 %copy-start.1 = (f32[3,64,64]{2,1,0:T(8,128)S(1)}, f32[3,64,64]{2,1,0:T(8,128)}, u32[]{:S(2)}) copy-start(f32[3,64,64]{2,1,0:T(8,128)} %param.16) | copy-start | bytes 147460
  6.5 69.1 %all-to-all-start = ((f32[1056,4,128]{2,1,0:T(4,128)}), f32[1056,4,128]{2,1,0:T(4,128)S(1)}, u32[]{:S(2)}, u32[]{:S(2)}) async-start(f32[1056,4,128]{2,1,0:T(4,128)} %pack_rows.1), calls=%async_computation | async-start | bytes 4325376 | tf_op jit(solution)/shard_map/all_to_all | solution.py:614
  74.8 23.2 %copy-start.3 = (f32[8,128]{1,0:T(8,128)S(1)}, f32[8,128]{1,0:T(8,128)}, u32[]{:S(2)}) copy-start(f32[8,128]{1,0:T(8,128)} %get-tuple-element.10) | copy-start | bytes 12292
  75.7 2.6 %copy-start = (f32[1056,4,128]{2,1,0:T(4,128)}, f32[1056,4,128]{2,1,0:T(4,128)S(1)}, u32[]{:S(2)}) copy-start(f32[1056,4,128]{2,1,0:T(4,128)S(1)} %all-to-all-done.rows_ref) | copy-start | bytes 6488068
  142.4 12.3 %copy-start.2 = (f32[2,8,128]{2,1,0:T(8,128)S(1)}, f32[2,8,128]{2,1,0:T(8,128)}, u32[]{:S(2)}) copy-start(f32[2,8,128]{2,1,0:T(8,128)} %get-tuple-element.13) | copy-start | bytes 24580
  142.5 12.3 %copy-start.4 = (f32[2]{0:T(128)S(1)}, f32[2]{0:T(128)}, u32[]{:S(2)}) copy-start(f32[2]{0:T(128)} %constant.11) | copy-start | bytes 28
